TPU v7x, 32 devices: a whole 2x2x4 slice. The times are simulated.
32 devices in a mesh: shard: 4 (over x, core), rep: 8 (over z, y).
Axes of the slice: x: 2, y: 2, z: 4, core: 2. Of those that a mesh axis runs over, the one named last changes fastest.
Arguments:
- block_input: bfloat16 [8, 512, 768], P('rep', 'shard'), may hold values from -6 to 6
- positions: int32 [8, 512], P('rep', 'shard'), may hold values from 0 to 1022, as said below
- segments: int32 [8, 512], P('rep'), may hold values from 0 to 6, as said below
- w_qkv: bfloat16 [768, 2304], P('shard')
- b_qkv: bfloat16 [2304], P('shard'), may hold values from -3 to 3
- w_out: bfloat16 [768, 768], P('shard'), may hold values from -0.875 to 0.875
- b_out: bfloat16 [768], P('shard'), may hold values from -3 to 3
- w_up: bfloat16 [768, 3072], P('shard'), may hold values from -0.21875 to 0.21875
- b_up: bfloat16 [3072], P('shard'), may hold values from -3 to 3
- w_down: bfloat16 [3072, 768], P('shard'), may hold values from -0.109375 to 0.109375
- b_down: bfloat16 [768], P('shard'), may hold values from -3 to 3
- ln1_gain: bfloat16 [768], P('shard'), may hold values from 0.5 to 1.5
- ln1_bias: bfloat16 [768], P('shard'), may hold values from -2 to 2
- ln2_gain: bfloat16 [768], P('shard'), may hold values from 0.5 to 1.5
- ln2_bias: bfloat16 [768], P('shard'), may hold values from -2 to 2
- cotangent: bfloat16 [8, 512, 768], P('rep', 'shard'), may hold values from -6 to 6
Outputs:
- output: float32 [8, 512, 768], P('rep', 'shard')
- input_grad: float32 [8, 512, 768], P('rep', 'shard')
- grad_w_qkv: float32 [768, 2304], P('shard')
- grad_b_qkv: float32 [2304], P('shard')
- grad_w_out: float32 [768, 768], P('shard')
- grad_b_out: float32 [768], P('shard')
- grad_w_up: float32 [768, 3072], P('shard')
- grad_b_up: float32 [3072], P('shard')
- grad_w_down: float32 [3072, 768], P('shard')
- grad_b_down: float32 [768], P('shard')
- grad_ln1_gain: float32 [768], P('shard')
- grad_ln1_bias: float32 [768], P('shard')
- grad_ln2_gain: float32 [768], P('shard')
- grad_ln2_bias: float32 [768], P('shard')
Inputs may be any that keep to these rules, and one draw needn't show every extreme that they name: `segments`: a token's document number within its sequence: 0 at the sequence's first token, one more at each document start; every document that starts inside a sequence has 102 tokens or more. `positions`: a token's position within its document, one more than that of the token before it inside the same document, 0 at a document's first token; a sequence's first document may have begun in an earlier sequence.
All inputs are finite; a program needn't handle non-finite values.
Results may differ from a plain program's by a relative error of at most 0.011.
Values may be sent and summed in bfloat16 or wider, within the bound.
No kernel may reach another device: no remote copies, remote signals or barrier semaphores. Data moves between devices by JAX's collectives and lax.ppermute only.
A program may use at most 128 MiB of HBM per device.

v0:
```python
import math

import jax
import jax.numpy as jnp
from jax import lax
from jax.experimental import pallas as pl
from jax.experimental.pallas import tpu as pltpu
from jax.sharding import PartitionSpec as P


HEAD_DIM = 64
ROT = 16

EPSILON = 1e-05
INV_ROOT_TWO = 0.7071067811865476
INV_ROOT_TWO_PI = 0.3989422804014327


BF = jnp.bfloat16
F32 = jnp.float32


def as_float(array_in):
    return array_in.astype(F32)


def dot(left, right, dims):
    return lax.dot_general(left, right, (dims, ((), ())), preferred_element_type=F32)


def normalize(values):
    centre = values - jnp.mean(values, axis=-1, keepdims=True)
    inv_std = lax.rsqrt(jnp.mean(centre * centre, axis=-1, keepdims=True) + EPSILON)
    return (centre * inv_std, inv_std)


def gelu_parts(pre_act):
    cdf = 0.5 * (1.0 + lax.erf(pre_act * INV_ROOT_TWO))
    return pre_act * cdf, cdf + pre_act * jnp.exp(-0.5 * pre_act * pre_act) * INV_ROOT_TWO_PI


def swap(value, axis, size, bit):
    return lax.ppermute(value, axis, [(i, i ^ bit) for i in range(size)])


def powers(size):
    return [1 << k for k in range(size.bit_length() - 1)]


def cube_gather(value, axis, size):
    buf, order = value[None], [0]
    for bit in reversed(powers(size)):
        buf = jnp.concatenate([buf, swap(buf, axis, size, bit)])
        order = order + [j ^ bit for j in order]
    return buf, order


def cube_scatter(value, axis, size):
    for bit in powers(size):
        half = value.shape[0] // 2
        value = value[:half] + swap(value[half:], axis, size, bit)
    return value[0]


def absolute(blocks, order, me):
    place = {off: k for k, off in enumerate(order)}
    table = jnp.array([place[i] for i in range(len(order))], jnp.int32)
    idx = table[jnp.arange(len(order)) ^ me]
    return jnp.stack([lax.dynamic_index_in_dim(blocks, idx[i], 0, False) for i in range(len(order))])


def call(kernel, outs, ins, scratch=(), flops=0, limit=8):
    shapes = [jax.ShapeDtypeStruct(s, d) for s, d in outs]
    moved = sum(math.prod(v.shape) * v.dtype.itemsize for v in [*ins, *shapes])
    return pl.pallas_call(
        kernel,
        out_shape=shapes,
        scratch_shapes=[pltpu.VMEM(s, d) for s, d in scratch],
        compiler_params=pltpu.CompilerParams(vmem_limit_bytes=limit * 1024 * 1024),
        cost_estimate=pl.CostEstimate(flops=flops, bytes_accessed=moved, transcendentals=0),
    )(*ins)


def bit_of(axis, bit):
    return jnp.where((lax.axis_index(axis) & bit) != 0, 1, 0).astype(jnp.int32)


def pack_kernel(wq, wu, q0, q1, q2, q3, u0, u1, u2, u3, scr):
    me = lax.axis_index("shard")
    rows = wq.shape[0]
    width = wq.shape[1] // 3
    wide = u0.shape[1]
    n_h = rows // HEAD_DIM
    for t in range(4):
        base = rows * t
        for h in range(n_h):
            a = base + HEAD_DIM * h
            scr[t, :, 2 * HEAD_DIM * h : 2 * HEAD_DIM * h + HEAD_DIM] = wq[:, a : a + HEAD_DIM]
            scr[t, :, 2 * HEAD_DIM * h + HEAD_DIM : 2 * HEAD_DIM * (h + 1)] = wq[
                :, width + a : width + a + HEAD_DIM
            ]
        scr[t, :, 2 * rows : 3 * rows] = wq[:, 2 * width + base : 2 * width + base + rows]
    for k, (q, u) in enumerate(((q0, u0), (q1, u1), (q2, u2), (q3, u3))):
        t = me ^ k
        q[...] = scr[t]
        u[...] = wu[:, pl.ds(pl.multiple_of(t * wide, 128), wide)]


def normed_of(ref):
    return normalize(ref[...].astype(F32))[0]


def write_rows(targets, grid, first, second, place):
    for target, half, b in zip(
        targets, (1 - first, 1 - first, first, first), (1 - second, second, 1 - second, second)
    ):
        n_t, n_r, _ = target.shape
        for t in range(n_t):
            start = pl.multiple_of(place(half, b, t), 16)
            target[t] = grid[pl.ds(start, n_r), :]


def att_kernel(order, x0, x1, x2, x3, c0, c1, c2, c3, q0, q1, q2, q3, gain, bias, bq, ca, sa, sb,
               segc, segr, idc, idr, wo,
               sa_o, sb_o, ka_o, kb_o, att_o, dproj_o, wfull, bsum, csum, hid, cot, grid, neg):
    me = lax.axis_index("shard")
    first, second = (bit_of("rep", bit) for bit in order)
    rows, width = wo.shape
    count = x0.shape[0]
    n_h = rows // HEAD_DIM
    for j, (x, c, q) in enumerate(((x0, c0, q0), (x1, c1, q1), (x2, c2, q2), (x3, c3, q3))):
        hid[count * j : count * (j + 1), :] = (normed_of(x) * gain[...] + bias[...]).astype(BF)
        cot[count * j : count * (j + 1), :] = c[...]
        wfull[pl.ds(pl.multiple_of((me ^ j) * rows, 16), rows), :] = q[...]
    allowed = (idr[...] <= idc[...]) & (segc[...] == segr[...])
    neg[...] = jnp.where(allowed, 0.0, -jnp.inf)
    proj = dot(hid[...], wfull[...], ((1,), (0,))) + bq[...]
    d_att = dot(cot[...], wo[...], ((1,), (1,))).astype(BF)
    for h in range(n_h):
        two = 2 * HEAD_DIM
        qk = proj[:, two * h : two * (h + 1)]
        qk = qk * ca[...] + pltpu.roll(qk, two - ROT // 2, 1) * sa[...] + pltpu.roll(qk, ROT // 2, 1) * sb[...]
        qk = qk.astype(BF)
        query, key = qk[:, :HEAD_DIM], qk[:, HEAD_DIM:]
        vals = slice(2 * rows + HEAD_DIM * h, 2 * rows + HEAD_DIM * (h + 1))
        val = proj[:, vals].astype(BF)
        da = d_att[:, HEAD_DIM * h : HEAD_DIM * (h + 1)]
        scores = dot(query, key, ((1,), (1,))) * 0.125 + neg[...]
        top = jnp.max(scores, axis=-1, keepdims=True)
        expo = jnp.exp(scores - top)
        prob = expo * (1.0 / jnp.sum(expo, axis=-1, keepdims=True))
        prob_b = prob.astype(BF)
        att = dot(prob_b, val, ((1,), (0,))).astype(BF)
        att_o[:, HEAD_DIM * h : HEAD_DIM * (h + 1)] = att
        d_val = dot(prob_b, da, ((0,), (0,)))
        d_prob = dot(da, val, ((1,), (1,)))
        row_dot = jnp.sum(as_float(da) * as_float(att), axis=-1, keepdims=True)
        d_score = (prob * (d_prob - row_dot) * 0.125).astype(BF)
        dqk = jnp.concatenate(
            [dot(d_score, key, ((1,), (0,))), dot(d_score, query, ((0,), (0,)))], axis=1
        )
        dqk = dqk * ca[...] - pltpu.roll(dqk, two - ROT // 2, 1) * sa[...] - pltpu.roll(dqk, ROT // 2, 1) * sb[...]
        dproj_o[:, two * h : two * (h + 1)] = dqk.astype(BF)
        dproj_o[:, vals] = d_val.astype(BF)
        bsum[:, two * h : two * (h + 1)] = jnp.sum(dqk, axis=0, keepdims=True)
        bsum[:, vals] = jnp.sum(d_val, axis=0, keepdims=True)
    csum[...] = jnp.sum(as_float(cot[...]), axis=0, keepdims=True)
    grid[:, : 3 * rows] = dot(hid[...], dproj_o[...], ((0,), (0,))).astype(BF)
    g_out = dot(att_o[...], cot[...], ((0,), (0,))).astype(BF)
    for t in range(width // rows):
        grid[rows * t : rows * (t + 1), 3 * rows :] = g_out[:, rows * t : rows * (t + 1)]
    n_r = sa_o.shape[1]
    write_rows(
        (sa_o, sb_o, ka_o, kb_o), grid, first, second, lambda half, b, t: t * rows + (2 * half + b) * n_r
    )


def mlp1_kernel(order, x0, x1, x2, x3, c0, c1, c2, c3, u0, u1, u2, u3, gain, bias, bup,
                sa_o, sb_o, ka_o, kb_o, hid, activ, slope, wfull, cot, grid):
    me = lax.axis_index("shard")
    first, second = (bit_of("rep", bit) for bit in order)
    count = x0.shape[0]
    rows = u0.shape[0]
    for j, (x, c, u) in enumerate(((x0, c0, u0), (x1, c1, u1), (x2, c2, u2), (x3, c3, u3))):
        hid[count * j : count * (j + 1), :] = (normed_of(x) * gain[...] + bias[...]).astype(BF)
        cot[count * j : count * (j + 1), :] = c[...]
        wfull[pl.ds(pl.multiple_of((me ^ j) * rows, 16), rows), :] = u[...]
    for j in range(4):
        part = slice(count * j, count * (j + 1))
        pre_act = dot(hid[part, :], wfull[...], ((1,), (0,))) + bup[...]
        act, slp = gelu_parts(pre_act)
        activ[part, :] = act.astype(BF)
        slope[part, :] = slp
    grid[...] = dot(activ[...], cot[...], ((0,), (0,))).astype(BF)
    n_t, n_r, _ = sa_o.shape
    write_rows(
        (sa_o, sb_o, ka_o, kb_o), grid, first, second, lambda half, b, t: ((half * 2 + b) * n_t + t) * n_r
    )


def mlp2_kernel(order, c0, c1, c2, c3, hid, slope, wd, sa_o, sb_o, ka_o, kb_o, dpre, bsum, grid):
    first, second = (bit_of("rep", bit) for bit in order)
    count = c0.shape[0]
    total = None
    for j, c in enumerate((c0, c1, c2, c3)):
        part = slice(count * j, count * (j + 1))
        d_pre = dot(c[...], wd[...], ((1,), (1,))) * slope[part, :]
        dpre[part, :] = d_pre.astype(BF)
        piece = jnp.sum(d_pre, axis=0, keepdims=True)
        total = piece if total is None else total + piece
    bsum[...] = total
    grid[...] = dot(hid[...], dpre[...], ((0,), (0,))).astype(BF)
    n_r = sa_o.shape[1]
    rows = n_r * 4
    write_rows(
        (sa_o, sb_o, ka_o, kb_o), grid, first, second, lambda half, b, t: t * rows + (2 * half + b) * n_r
    )


def mlp3_kernel(x0, x1, x2, x3, att, activ, dproj, dpre, wo, wd, wq, wu, gain1, gain2,
                send, keep, sums):
    count = x0.shape[0]
    total = [None] * 4
    for j, x in enumerate((x0, x1, x2, x3)):
        part = slice(count * j, count * (j + 1))
        out = dot(att[part, :], wo[...], ((1,), (0,))) + dot(activ[part, :], wd[...], ((1,), (0,)))
        one = dot(dproj[part, :], wq[...], ((1,), (1,)))
        two = dot(dpre[part, :], wu[...], ((1,), (1,)))
        normed = normed_of(x)
        target = keep if j % 2 == 0 else send
        target[j // 2, 0] = out.astype(BF)
        target[j // 2, 1] = (one * gain1[...] + two * gain2[...]).astype(BF)
        for k, value in enumerate((one * normed, one, two * normed, two)):
            piece = jnp.sum(value, axis=0, keepdims=True)
            total[k] = piece if total[k] is None else total[k] + piece
    for k in range(4):
        sums[k : k + 1, :] = total[k]


def add_kernel(kept, got, out):
    out[...] = (as_float(kept[...]) + as_float(got[...])).astype(out.dtype)


def add_split_kernel(bit, kept, got, more, send, keep):
    mine = bit_of("rep", bit)
    for place, out in ((1 - mine, send), (mine, keep)):
        out[...] = (as_float(kept[place]) + as_float(got[place]) + as_float(more[place])).astype(BF)


def add_pieces_kernel(kept, got, more, p0, p1, p2, p3, *rest):
    me = lax.axis_index("shard")
    cols = p0.shape[1]
    for k, p in enumerate((p0, p1, p2, p3)):
        t = me ^ k
        total = (as_float(kept[t]) + as_float(got[t]) + as_float(more[t])).astype(BF)
        p[...] = total[:, :cols]
        if rest:
            rest[0][t] = total[:, cols:]


def pieces_split_kernel(bit, p0, p1, p2, p3, *rest):
    me = lax.axis_index("shard")
    mine = bit_of("rep", bit)
    send, keep = rest[-2:]
    cols = p0.shape[1]
    for k, p in enumerate((p0, p1, p2, p3)):
        s = me ^ k
        pair, slot = s >> 1, s & 1
        for target, wanted in ((keep, mine), (send, 1 - mine)):

            @pl.when(pair == wanted)
            def _(target=target):
                target[slot, :, :cols] = p[...]
                if len(rest) > 2:
                    target[slot, :, cols:] = rest[0][s]


def pair_kernel(bit, own, got, out):
    mine = bit_of("rep", bit)
    out[mine] = own[...]
    out[1 - mine] = got[...]


def quarters(order, refs):
    first, second = (bit_of("rep", bit) for bit in order)
    return zip(refs, (first, first, 1 - first, 1 - first), (second, 1 - second, second, 1 - second))


def final_down_kernel(order, p0, p1, p2, p3, out):
    for value, half, b in quarters(order, (p0, p1, p2, p3)):
        n_t, n_r, _ = value.shape
        for t in range(n_t):
            start = pl.multiple_of(((half * 2 + b) * n_t + t) * n_r, 8)
            out[pl.ds(start, n_r), :] = as_float(value[t])


def final_up_kernel(order, p0, p1, p2, p3, out):
    for value, half, b in quarters(order, (p0, p1, p2, p3)):
        n_s, n_r, wide = value.shape
        start = pl.multiple_of((half * 2 + b) * n_r, 8)
        for s in range(n_s):
            out[pl.ds(start, n_r), wide * s : wide * (s + 1)] = as_float(value[s])


def final_qkv_kernel(order, p0, p1, p2, p3, out, out_w):
    rows = out_w.shape[0]
    n_h = rows // HEAD_DIM
    for value, half, b in quarters(order, (p0, p1, p2, p3)):
        n_s, n_r, width = value.shape
        place = pl.ds(pl.multiple_of((half * 2 + b) * n_r, 8), n_r)
        for s in range(n_s):
            block = as_float(value[s])
            for h in range(n_h):
                a = rows * s + HEAD_DIM * h
                two = 2 * HEAD_DIM * h
                out[place, a : a + HEAD_DIM] = block[:, two : two + HEAD_DIM]
                out[place, width + a : width + a + HEAD_DIM] = block[:, two + HEAD_DIM : two + 2 * HEAD_DIM]
            out[place, 2 * width + rows * s : 2 * width + rows * (s + 1)] = block[:, 2 * rows : 3 * rows]
            out_w[place, rows * s : rows * (s + 1)] = block[:, 3 * rows :]


def make_body(shards, reps):
    def body(
        block_input,
        positions,
        segments,
        w_qkv,
        b_qkv,
        w_out,
        b_out,
        w_up,
        b_up,
        w_down,
        b_down,
        ln1_gain,
        ln1_bias,
        ln2_gain,
        ln2_bias,
        cotangent,
    ):
        me = lax.axis_index("shard")
        tokens_in = block_input[0]
        cotan_own = cotangent[0]
        count, width = tokens_in.shape
        length = segments.shape[1]
        rows = w_qkv.shape[0]
        wide = w_up.shape[1] // shards
        bits = powers(reps)

        def to(j, value):
            return swap(value, "shard", shards, j)

        def gather(value):
            two = to(2, value)
            one = to(1, value)
            return value, one, two, swap(two, "shard", shards, 1)

        x = gather(tokens_in)
        packed = call(
            pack_kernel,
            [((rows, 3 * rows), BF)] * 4 + [((rows, wide), BF)] * 4,
            (w_qkv, w_up),
            scratch=[((4, rows, 3 * rows), BF)],
        )
        q_w = (packed[0], *(to(j, packed[j]) for j in (1, 2, 3)))
        c = gather(cotan_own)
        u_w = (packed[4], *(to(j, packed[4 + j]) for j in (1, 2, 3)))

        position = positions[0]
        small = jnp.concatenate(
            [
                ln1_gain,
                ln1_bias,
                ln2_gain,
                ln2_bias,
                b_out,
                b_down,
                b_qkv,
                (position >> 5).astype(BF),
                (position & 31).astype(BF),
            ]
        )
        small_rel, order = cube_gather(small, "shard", shards)
        small_abs = absolute(small_rel, order, me)
        cuts = [0]
        for part in (rows, rows, rows, rows, rows, rows, 3 * rows, count, count):
            cuts.append(cuts[-1] + part)
        pieces = [small_abs[:, a:b] for a, b in zip(cuts[:-1], cuts[1:])]
        gain_one, bias_one, gain_two, bias_two, full_bout, full_bdown = [
            as_float(p.reshape(1, -1)) for p in pieces[:6]
        ]
        own_b = lax.dynamic_slice_in_dim(pieces[6].reshape(3, width), me * rows, rows, 1)
        n_h = rows // HEAD_DIM
        bias_qkv = as_float(
            jnp.concatenate(
                [
                    own_b[:2].reshape(2, n_h, HEAD_DIM).transpose(1, 0, 2).reshape(-1),
                    own_b[2],
                ]
            )
        ).reshape(1, -1)
        digits = [small_rel[order.index(j)] for j in range(shards)]
        pos_rel = jnp.concatenate(
            [
                d[cuts[7] : cuts[8]].astype(jnp.int32) * 32 + d[cuts[8] : cuts[9]].astype(jnp.int32)
                for d in digits
            ]
        )
        places = jnp.concatenate(
            [(me ^ j) * count + jnp.arange(count, dtype=jnp.int32) for j in range(shards)]
        )
        seg_abs = segments[0].reshape(shards, count)
        seg_rel = jnp.concatenate(
            [lax.dynamic_index_in_dim(seg_abs, me ^ j, 0, False) for j in range(shards)]
        )
        half = ROT // 2
        lane = jnp.arange(2 * HEAD_DIM) % HEAD_DIM
        freqs = jnp.exp((lane % half).astype(F32) * (-math.log(10000.0) / half))
        angles = pos_rel.astype(F32)[:, None] * freqs[None, :]
        cosine, sine = jnp.cos(angles), jnp.sin(angles)
        ca = jnp.where(lane < ROT, cosine, 1.0)
        sa = jnp.where(lane < half, -sine, 0.0)
        sb = jnp.where((lane >= half) & (lane < ROT), sine, 0.0)

        first, second, third = bits[:3]
        order_att, order_down, order_up = (first, second), (first, second), (second, first)
        sub = rows // 4
        n_c = width // rows

        *grad_a, hid_two, activ, slope, wu_full = call(
            lambda *refs: mlp1_kernel(order_down, *refs),
            [((2, wide // 8, width), BF)] * 4
            + [((length, width), BF), ((length, wide), BF), ((length, wide), F32), ((width, wide), BF)],
            (*x, *c, *u_w, gain_two, bias_two, as_float(b_up).reshape(1, -1)),
            scratch=[((length, width), BF), ((wide, width), BF)],
            flops=2_000_000_000,
            limit=24,
        )
        *grad_b, dpre, bup_sum = call(
            lambda *refs: mlp2_kernel(order_up, *refs),
            [((shards, sub, wide), BF)] * 4 + [((length, wide), BF), ((1, wide), F32)],
            (*c, hid_two, slope, w_down),
            scratch=[((width, wide), BF)],
            flops=2_000_000_000,
            limit=24,
        )
        *grad_c, att, dproj, wq_full, bsum, csum = call(
            lambda *refs: att_kernel(order_att, *refs),
            [((n_c, sub, width), BF)] * 4
            + [
                ((length, rows), BF),
                ((length, 3 * rows), BF),
                ((width, 3 * rows), BF),
                ((1, 3 * rows), F32),
                ((1, width), F32),
            ],
            (*x, *c, *q_w, gain_one, bias_one, bias_qkv, ca, sa, sb,
             seg_rel[:, None], seg_rel[None, :], places[:, None], places[None, :], w_out),
            scratch=[((length, width), BF), ((length, width), BF), ((width, width), BF), ((length, length), F32)],
            flops=4_000_000_000,
            limit=24,
        )
        rs_send, rs_keep, ln_sums = call(
            mlp3_kernel,
            [((2, 2, count, width), BF)] * 2 + [((4, width), F32)],
            (*x, att, activ, dproj, dpre, w_out, w_down, wq_full, wu_full, gain_one, gain_two),
            flops=3_000_000_000,
            limit=24,
        )

        def over(bit, value):
            return swap(value, "rep", reps, bit)

        def start_sum(bit_order, grad):
            sent_a, sent_b, kept_a, kept_b = grad
            one, two = bit_order
            got_a = over(one, sent_a)
            got_b = over(one, sent_b)
            (sent,) = call(add_kernel, [(kept_a.shape, BF)], (kept_a, got_a))
            return kept_b, got_b, over(two, sent)

        def finish_sum(bit_order, sent, kept, shape):
            one, two = bit_order
            got = over(third, sent)
            (own,) = call(add_kernel, [(kept.shape, BF)], (kept, got))
            for bit in bits[3:]:
                more = over(bit, own)
                (own,) = call(add_kernel, [(own.shape, BF)], (own, more))
            (both,) = call(lambda *refs: pair_kernel(third, *refs), [((2, *own.shape), BF)], (own, over(third, own)))
            both = both.reshape(shape)
            other = over(two, both)
            return both, other, over(one, both), over(one, other)

        def shard_stream(bit_order, grad, cols):
            held = start_sum(bit_order, grad)
            shape = held[0].shape
            extra = [] if cols == shape[2] else [((n_c, sub, shape[2] - cols), BF)]
            parts = call(add_pieces_kernel, [((sub, cols), BF)] * 4 + extra, held)
            mixed = (parts[0], *(to(j, parts[j]) for j in range(1, 4)), *parts[4:])
            sent, kept = call(lambda *refs: pieces_split_kernel(third, *refs), [((2, sub, shape[2]), BF)] * 2, mixed)
            return finish_sum(bit_order, sent, kept, shape)

        def plain_stream(bit_order, grad):
            held = start_sum(bit_order, grad)
            shape = held[0].shape
            sent, kept = call(lambda *refs: add_split_kernel(third, *refs), [(shape[1:], BF)] * 2, held)
            return finish_sum(bit_order, sent, kept, shape)

        own_c = shard_stream(order_att, grad_c, 3 * rows)
        own_a = plain_stream(order_down, grad_a)
        own_b = shard_stream(order_up, grad_b, wide)
        tot_qkv, tot_out = call(
            lambda *refs: final_qkv_kernel(order_att, *refs), [((rows, 3 * width), F32), ((rows, width), F32)], own_c
        )
        (tot_down,) = call(lambda *refs: final_down_kernel(order_down, *refs), [((wide, width), F32)], own_a)
        (tot_up,) = call(lambda *refs: final_up_kernel(order_up, *refs), [((rows, shards * wide), F32)], own_b)

        got = to(1, rs_send)
        (onward,) = call(add_kernel, [(got.shape[1:], BF)], (rs_keep[1], got[1]))
        total = as_float(rs_keep[0]) + as_float(got[0]) + as_float(to(2, onward))
        output = as_float(tokens_in) + total[0] + full_bout + full_bdown
        d_norm = total[1]
        own_normed, inv_std = normalize(as_float(tokens_in))
        d_input = as_float(cotan_own) + inv_std * (
            d_norm
            - jnp.mean(d_norm, axis=-1, keepdims=True)
            - own_normed * jnp.mean(d_norm * own_normed, axis=-1, keepdims=True)
        )

        qk_sum = bsum[0, : 2 * rows].reshape(n_h, 2, HEAD_DIM).transpose(1, 0, 2).reshape(2, rows)
        grad_bqkv = jnp.concatenate([qk_sum, bsum[:, 2 * rows :]])
        spread = lax.dynamic_update_slice(jnp.zeros((3, width), F32), grad_bqkv, (0, me * rows))
        vec = jnp.concatenate(
            [ln_sums[k].reshape(shards, -1) for k in range(4)] + [spread.reshape(shards, -1)], axis=1
        )
        vec_rel = jnp.stack([lax.dynamic_index_in_dim(vec, me ^ j, 0, False) for j in order])
        mine = cube_scatter(vec_rel, "shard", shards)
        cot_sum = lax.dynamic_slice_in_dim(csum[0], me * rows, rows)
        mine = jnp.concatenate([mine, cot_sum, bup_sum[0]])
        mine = mine.reshape(1, -1)
        for bit in bits:
            (mine,) = call(add_kernel, [(mine.shape, F32)], (mine, over(bit, mine)), limit=1)
        mine = mine.reshape(-1)
        g1, bb1, g2, bb2 = [mine[k * rows : (k + 1) * rows] for k in range(4)]
        tot_bqkv = mine[4 * rows : 7 * rows]
        tot_cot = mine[7 * rows : 8 * rows]
        tot_bup = mine[8 * rows :]
        return (
            output[None],
            d_input[None],
            tot_qkv,
            tot_bqkv,
            tot_out,
            tot_cot,
            tot_up,
            tot_bup,
            tot_down,
            tot_cot,
            g1,
            bb1,
            g2,
            bb2,
        )

    return body


def solution(mesh):
    body = make_body(mesh.shape["shard"], mesh.shape["rep"])
    return jax.shard_map(
        body,
        mesh=mesh,
        in_specs=(
            P("rep", "shard", None),
            P("rep", "shard"),
            P("rep", None),
            P("shard", None),
            P("shard"),
            P("shard", None),
            P("shard"),
            P("shard", None),
            P("shard"),
            P("shard", None),
            P("shard"),
            P("shard"),
            P("shard"),
            P("shard"),
            P("shard"),
            P("rep", "shard", None),
        ),
        out_specs=(
            P("rep", "shard", None),
            P("rep", "shard", None),
            P("shard", None),
            P("shard"),
            P("shard", None),
            P("shard"),
            P("shard", None),
            P("shard"),
            P("shard", None),
            P("shard"),
            P("shard"),
            P("shard"),
            P("shard"),
            P("shard"),
        ),
        check_vma=False,
    )
```

profile of v0, /device:TPU:0, one launch (start us, length us, event | category | flops | bytes accessed | tf_op | source)
XLA Modules:
  0.0 194.1 jit_solution(12310058603949423133)
XLA Ops:
  1.2 2.6 %collective-permute-start.1 = (bf16[128,768]{1,0:T(8,128)(2,1)}, bf16[128,768]{1,0:T(8,128)(2,1)}, u32[]{:S(2)}, u32[]{:S(2)}) collective-permute-start(bf16[128,768]{1,0:T(8,128)(2,1)} %bitcast.59), channel_id=1, source_target_pairs={{0,16},{8,24},{16,0},{24,8},{1,17},{9,25},{17,1},{25,9},{2,18},{10... | collective-permute-start | bytes 589832 | tf_op jit(solution)/shard_map/ppermute | solution.py:43
  4.9 4.8 %concatenate.46 = bf16[1984]{0:T(1024)(128)(2,1)S(1)} concatenate(bf16[192]{0:T(256)(128)(2,1)} %param.28, bf16[192]{0:T(256)(128)(2,1)} %param.29, bf16[192]{0:T(256)(128)(2,1)} %param.30, bf16[192]{0:T(256)(128)(2,1)} %param.31, bf16[192]{0:T(256)(128)(2,1)} %param.23, bf16[192]{0:T(256)(128)(2,1)} %param.27, bf16[576]{0:T(1024)(128)(2,1)} %param.21, ...), dimensions={0} | concatenate | bytes 7936 | tf_op jit(solution)/shard_map/concatenate | solution.py:370
  34.8 5.1 %collective-permute-done.7.refs_10_ = bf16[192,576]{1,0:T(8,128)(2,1)S(1)} collective-permute-done((bf16[192,576]{1,0:T(8,128)(2,1)S(1)}, bf16[192,576]{1,0:T(8,128)(2,1)S(1)}, u32[]{:S(2)}, u32[]{:S(2)}) %collective-permute-start.7) | collective-permute-done | bytes 221216 | tf_op jit(solution)/shard_map/ppermute | solution.py:43
  40.2 3.7 %collective-permute-done.8.refs_11_ = bf16[192,576]{1,0:T(8,128)(2,1)S(1)} collective-permute-done((bf16[192,576]{1,0:T(8,128)(2,1)S(1)}, bf16[192,576]{1,0:T(8,128)(2,1)S(1)}, u32[]{:S(2)}, u32[]{:S(2)}) %collective-permute-start.8) | collective-permute-done | bytes 221216 | tf_op jit(solution)/shard_map/ppermute | solution.py:43
  45.8 8.9 %shard_map.273 = (bf16[4,48,768]{2,1,0:T(8,128)(2,1)S(1)}, bf16[4,48,768]{2,1,0:T(8,128)(2,1)S(1)}, bf16[4,48,768]{2,1,0:T(8,128)(2,1)S(1)}, bf16[4,48,768]{2,1,...) custom-call(bf16[128,768]{1,0:T(8,128)(2,1)S(1)} %bitcast.60, ...), custom_call_target="tpu_custom_call" | custom-call | flops 4000000000 | bytes 6411776 | tf_op jit(solution)/shard_map/pallas_call | solution.py:75
  56.5 4.6 %shard_map.274 = (bf16[2,96,768]{2,1,0:T(8,128)(2,1)S(1)}, bf16[2,96,768]{2,1,0:T(8,128)(2,1)}, bf16[2,96,768]{2,1,0:T(8,128)(2,1)S(1)}, bf16[2,96,768]{2,1,0:T(...) custom-call(bf16[128,768]{1,0:T(8,128)(2,1)S(1)} %bitcast.61, ...), custom_call_target="tpu_custom_call" | custom-call | flops 2000000000 | bytes 8266752 | tf_op jit(solution)/shard_map/pallas_call | solution.py:75
  61.2 3.5 %shard_map.275 = (bf16[4,48,768]{2,1,0:T(8,128)(2,1)S(1)}, bf16[4,48,768]{2,1,0:T(8,128)(2,1)S(1)}, bf16[4,48,768]{2,1,0:T(8,128)(2,1)S(1)}, bf16[4,48,768]{2,1,...) custom-call(bf16[128,768]{1,0:T(8,128)(2,1)S(1)} %bitcast.73, ...), custom_call_target="tpu_custom_call" | custom-call | flops 2000000000 | bytes 6294528 | tf_op jit(solution)/shard_map/pallas_call | solution.py:75
  66.2 4.7 %shard_map.276 = (bf16[2,2,128,768]{3,2,1,0:T(8,128)(2,1)S(1)}, bf16[2,2,128,768]{3,2,1,0:T(8,128)(2,1)S(1)}, f32[4,768]{1,0:T(4,128)S(1)}) custom-call(bf16[128,768]{1,0:T(8,128)(2,1)S(1)} %bitcast.62, bf16[128,768]{1,0:T(8,128)(2,1)S(1)} %copy-done.22, bf16[128,768]{1,0:T(8,128)(2,1)} %collective-permute-done.1.refs_2_.x2, ...), custom_call_target="tpu_custom_call" | custom-call | flops 3000000000 | bytes 8275968 | tf_op jit(solution)/shard_map/pallas_call | solution.py:75
  78.7 2.8 %collective-permute-done.28 = f32[1,1344]{1,0:T(1,128)} collective-permute-done((f32[1,1344]{1,0:T(1,128)}, f32[1,1344]{1,0:T(1,128)}, u32[]{:S(2)}, u32[]{:S(2)}) %collective-permute-start.28) | collective-permute-done | bytes 5408 | tf_op jit(solution)/shard_map/ppermute | solution.py:43
  85.2 3.9 %collective-permute-done.29.got = f32[1,2304]{1,0:T(1,128)S(1)} collective-permute-done((f32[1,2304]{1,0:T(1,128)S(1)}, f32[1,2304]{1,0:T(1,128)S(1)}, u32[]{:S(2)}, u32[]{:S(2)}) %collective-permute-start.29) | collective-permute-done | bytes 9248 | tf_op jit(solution)/shard_map/ppermute | solution.py:43
  92.7 2.6 %collective-permute-start.31 = (f32[1,2304]{1,0:T(1,128)S(1)}, f32[1,2304]{1,0:T(1,128)S(1)}, u32[]{:S(2)}, u32[]{:S(2)}) collective-permute-start(f32[1,2304]{1,0:T(1,128)S(1)} %shard_map.285.kept), channel_id=1, source_target_pairs={{0,4},{1,5},{2,6},{3,7},{4,0},{5,1},{6,2},{7,3},{8,12},{9,13},{10,... | collective-permute-start | bytes 27656 | tf_op jit(solution)/shard_map/ppermute | solution.py:43
  101.7 2.9 %collective-permute-done.18.more = bf16[4,48,768]{2,1,0:T(8,128)(2,1)S(1)} collective-permute-done((bf16[4,48,768]{2,1,0:T(8,128)(2,1)S(1)}, bf16[4,48,768]{2,1,0:T(8,128)(2,1)S(1)}, u32[]{:S(2)}, u32[]{:S(2)}) %collective-permute-start.18) | collective-permute-done | bytes 294944 | tf_op jit(solution)/shard_map/ppermute | solution.py:43
  104.7 2.5 %collective-permute-start.45 = (bf16[2,96,768]{2,1,0:T(8,128)(2,1)S(1)}, bf16[2,96,768]{2,1,0:T(8,128)(2,1)S(1)}, u32[]{:S(2)}, u32[]{:S(2)}) collective-permute-start(bf16[2,96,768]{2,1,0:T(8,128)(2,1)S(1)} %shard_map.293), channel_id=1, source_target_pairs={{0,2},{1,3},{2,0},{3,1},{4,6},{5,7},{6,4},{7,5},{8,10},{9,11},{10,... | collective-permute-start | bytes 884744 | tf_op jit(solution)/shard_map/ppermute | solution.py:43
  108.7 2.3 %collective-permute-done.32.got = bf16[4,48,768]{2,1,0:T(8,128)(2,1)S(1)} collective-permute-done((bf16[4,48,768]{2,1,0:T(8,128)(2,1)S(1)}, bf16[4,48,768]{2,1,0:T(8,128)(2,1)S(1)}, u32[]{:S(2)}, u32[]{:S(2)}) %collective-permute-start.32) | collective-permute-done | bytes 294944 | tf_op jit(solution)/shard_map/ppermute | solution.py:43
  129.0 8.2 %collective-permute-done.46.got = bf16[96,768]{1,0:T(8,128)(2,1)S(1)} collective-permute-done((bf16[96,768]{1,0:T(8,128)(2,1)S(1)}, bf16[96,768]{1,0:T(8,128)(2,1)S(1)}, u32[]{:S(2)}, u32[]{:S(2)}) %collective-permute-start.46) | collective-permute-done | bytes 147488 | tf_op jit(solution)/shard_map/ppermute | solution.py:43
  137.4 6.2 %collective-permute-done.22.got = bf16[2,48,768]{2,1,0:T(8,128)(2,1)S(1)} collective-permute-done((bf16[2,48,768]{2,1,0:T(8,128)(2,1)S(1)}, bf16[2,48,768]{2,1,0:T(8,128)(2,1)S(1)}, u32[]{:S(2)}, u32[]{:S(2)}) %collective-permute-start.22) | collective-permute-done | bytes 147488 | tf_op jit(solution)/shard_map/ppermute | solution.py:43
  143.7 3.0 %collective-permute-done.38.got = bf16[2,48,768]{2,1,0:T(8,128)(2,1)S(1)} collective-permute-done((bf16[2,48,768]{2,1,0:T(8,128)(2,1)S(1)}, bf16[2,48,768]{2,1,0:T(8,128)(2,1)S(1)}, u32[]{:S(2)}, u32[]{:S(2)}) %collective-permute-start.38) | collective-permute-done | bytes 147488 | tf_op jit(solution)/shard_map/ppermute | solution.py:43
  148.1 5.0 %collective-permute-done.47.refs_1_ = bf16[96,768]{1,0:T(8,128)(2,1)S(1)} collective-permute-done((bf16[96,768]{1,0:T(8,128)(2,1)S(1)}, bf16[96,768]{1,0:T(8,128)(2,1)S(1)}, u32[]{:S(2)}, u32[]{:S(2)}) %collective-permute-start.47) | collective-permute-done | bytes 147488 | tf_op jit(solution)/shard_map/ppermute | solution.py:43
  153.1 3.4 %collective-permute-start.48 = (bf16[2,96,768]{2,1,0:T(8,128)(2,1)S(1)}, bf16[2,96,768]{2,1,0:T(8,128)(2,1)S(1)}, u32[]{:S(2)}, u32[]{:S(2)}) collective-permute-start(bf16[2,96,768]{2,1,0:T(8,128)(2,1)S(1)} %shard_map.296.refs_0_), channel_id=1, source_target_pairs={{0,2},{1,3},{2,0},{3,1},{4,6},{5,7},{6,4},{7,5},{8,10},{9,11},{10,... | collective-permute-start | bytes 884744 | tf_op jit(solution)/shard_map/ppermute | solution.py:43
  159.6 2.6 %collective-permute-done.39.refs_1_ = bf16[2,48,768]{2,1,0:T(8,128)(2,1)S(1)} collective-permute-done((bf16[2,48,768]{2,1,0:T(8,128)(2,1)S(1)}, bf16[2,48,768]{2,1,0:T(8,128)(2,1)S(1)}, u32[]{:S(2)}, u32[]{:S(2)}) %collective-permute-start.39) | collective-permute-done | bytes 147488 | tf_op jit(solution)/shard_map/ppermute | solution.py:43
  169.3 4.8 %collective-permute-done.24.refs_1_ = bf16[4,48,768]{2,1,0:T(8,128)(2,1)S(1)} collective-permute-done((bf16[4,48,768]{2,1,0:T(8,128)(2,1)S(1)}, bf16[4,48,768]{2,1,0:T(8,128)(2,1)S(1)}, u32[]{:S(2)}, u32[]{:S(2)}) %collective-permute-start.24) | collective-permute-done | bytes 294944 | tf_op jit(solution)/shard_map/ppermute | solution.py:43
  175.6 2.9 %collective-permute-done.40.refs_1_ = bf16[4,48,768]{2,1,0:T(8,128)(2,1)S(1)} collective-permute-done((bf16[4,48,768]{2,1,0:T(8,128)(2,1)S(1)}, bf16[4,48,768]{2,1,0:T(8,128)(2,1)S(1)}, u32[]{:S(2)}, u32[]{:S(2)}) %collective-permute-start.40) | collective-permute-done | bytes 294944 | tf_op jit(solution)/shard_map/ppermute | solution.py:43
  180.1 4.6 %collective-permute-done.50.refs_3_ = bf16[2,96,768]{2,1,0:T(8,128)(2,1)S(1)} collective-permute-done((bf16[2,96,768]{2,1,0:T(8,128)(2,1)S(1)}, bf16[2,96,768]{2,1,0:T(8,128)(2,1)S(1)}, u32[]{:S(2)}, u32[]{:S(2)}) %collective-permute-start.50) | collective-permute-done | bytes 294944 | tf_op jit(solution)/shard_map/ppermute | solution.py:43
  186.3 3.9 %collective-permute-done.26.refs_3_ = bf16[4,48,768]{2,1,0:T(8,128)(2,1)S(1)} collective-permute-done((bf16[4,48,768]{2,1,0:T(8,128)(2,1)S(1)}, bf16[4,48,768]{2,1,0:T(8,128)(2,1)S(1)}, u32[]{:S(2)}, u32[]{:S(2)}) %collective-permute-start.26) | collective-permute-done | bytes 294944 | tf_op jit(solution)/shard_map/ppermute | solution.py:43
  (248 shorter events, 85.5 us)
Async XLA Ops:
  0.7 30.3 %collective-permute-start = (bf16[128,768]{1,0:T(8,128)(2,1)}, bf16[128,768]{1,0:T(8,128)(2,1)S(1)}, u32[]{:S(2)}, u32[]{:S(2)}) collective-permute-start(bf16[128,768]{1,0:T(8,128)(2,1)} %bitcast.58), channel_id=1, source_target_pairs={{0,8},{8,0},{16,24},{24,16},{1,9},{9,1},{17,25},{25,17},{2,10},{10... | collective-permute-start | bytes 589832 | tf_op jit(solution)/shard_map/ppermute | solution.py:43
  1.2 30.1 %collective-permute-start.1 = (bf16[128,768]{1,0:T(8,128)(2,1)}, bf16[128,768]{1,0:T(8,128)(2,1)}, u32[]{:S(2)}, u32[]{:S(2)}) collective-permute-start(bf16[128,768]{1,0:T(8,128)(2,1)} %bitcast.59), channel_id=1, source_target_pairs={{0,16},{8,24},{16,0},{24,8},{1,17},{9,25},{17,1},{25,9},{2,18},{10... | collective-permute-start | bytes 589832 | tf_op jit(solution)/shard_map/ppermute | solution.py:43
  3.8 29.0 %collective-permute-start.3 = (bf16[128,768]{1,0:T(8,128)(2,1)}, bf16[128,768]{1,0:T(8,128)(2,1)}, u32[]{:S(2)}, u32[]{:S(2)}) collective-permute-start(bf16[128,768]{1,0:T(8,128)(2,1)} %bitcast.69), channel_id=1, source_target_pairs={{0,8},{8,0},{16,24},{24,16},{1,9},{9,1},{17,25},{25,17},{2,10},{10... | collective-permute-start | bytes 589832 | tf_op jit(solution)/shard_map/ppermute | solution.py:43
  3.9 29.3 %collective-permute-start.4 = (bf16[128,768]{1,0:T(8,128)(2,1)}, bf16[128,768]{1,0:T(8,128)(2,1)}, u32[]{:S(2)}, u32[]{:S(2)}) collective-permute-start(bf16[128,768]{1,0:T(8,128)(2,1)} %bitcast.70), channel_id=1, source_target_pairs={{0,16},{8,24},{16,0},{24,8},{1,17},{9,25},{17,1},{25,9},{2,18},{10... | collective-permute-start | bytes 589832 | tf_op jit(solution)/shard_map/ppermute | solution.py:43
  9.6 18.1 %collective-permute-start.9 = (bf16[1,1984]{1,0:T(2,128)(2,1)S(1)}, bf16[1,1984]{1,0:T(2,128)(2,1)S(1)}, u32[]{:S(2)}, u32[]{:S(2)}) collective-permute-start(bf16[1,1984]{1,0:T(2,128)(2,1)S(1)} %broadcast_in_dim.45), channel_id=1, source_target_pairs={{0,16},{8,24},{16,0},{24,8},{1,17},{9,25},{17,1},{25,9},{2,18},{10... | collective-permute-start | bytes 11912 | tf_op jit(solution)/shard_map/ppermute | solution.py:43
  34.3 20.4 %collective-permute-start.11 = (bf16[192,768]{1,0:T(8,128)(2,1)}, bf16[192,768]{1,0:T(8,128)(2,1)S(1)}, u32[]{:S(2)}, u32[]{:S(2)}) collective-permute-start(bf16[192,768]{1,0:T(8,128)(2,1)} %get-tuple-element.71), channel_id=1, source_target_pairs={{0,8},{8,0},{16,24},{24,16},{1,9},{9,1},{17,25},{25,17},{2,10},{10... | collective-permute-start | bytes 884744 | tf_op jit(solution)/shard_map/ppermute | solution.py:43
  39.9 14.9 %collective-permute-start.12 = (bf16[192,768]{1,0:T(8,128)(2,1)}, bf16[192,768]{1,0:T(8,128)(2,1)S(1)}, u32[]{:S(2)}, u32[]{:S(2)}) collective-permute-start(bf16[192,768]{1,0:T(8,128)(2,1)} %get-tuple-element.72), channel_id=1, source_target_pairs={{0,16},{8,24},{16,0},{24,8},{1,17},{9,25},{17,1},{25,9},{2,18},{10... | collective-permute-start | bytes 884744 | tf_op jit(solution)/shard_map/ppermute | solution.py:43
  73.3 22.0 %collective-permute-start.17 = (bf16[4,48,768]{2,1,0:T(8,128)(2,1)}, bf16[4,48,768]{2,1,0:T(8,128)(2,1)}, u32[]{:S(2)}, u32[]{:S(2)}) collective-permute-start(bf16[4,48,768]{2,1,0:T(8,128)(2,1)} %copy-done.16), channel_id=1, source_target_pairs={{0,1},{1,0},{2,3},{3,2},{4,5},{5,4},{6,7},{7,6},{8,9},{9,8},{10,11... | collective-permute-start | bytes 884744 | tf_op jit(solution)/shard_map/ppermute | solution.py:43
  74.8 23.3 %collective-permute-start.33 = (bf16[4,48,768]{2,1,0:T(8,128)(2,1)}, bf16[4,48,768]{2,1,0:T(8,128)(2,1)S(1)}, u32[]{:S(2)}, u32[]{:S(2)}) collective-permute-start(bf16[4,48,768]{2,1,0:T(8,128)(2,1)} %copy-done.18), channel_id=1, source_target_pairs={{0,2},{1,3},{2,0},{3,1},{4,6},{5,7},{6,4},{7,5},{8,10},{9,11},{10,... | collective-permute-start | bytes 884744 | tf_op jit(solution)/shard_map/ppermute | solution.py:43
  76.4 23.1 %collective-permute-start.44 = (bf16[2,96,768]{2,1,0:T(8,128)(2,1)}, bf16[2,96,768]{2,1,0:T(8,128)(2,1)S(1)}, u32[]{:S(2)}, u32[]{:S(2)}) collective-permute-start(bf16[2,96,768]{2,1,0:T(8,128)(2,1)} %copy-done.17), channel_id=1, source_target_pairs={{0,1},{1,0},{2,3},{3,2},{4,5},{5,4},{6,7},{7,6},{8,9},{9,8},{10,11... | collective-permute-start | bytes 884744 | tf_op jit(solution)/shard_map/ppermute | solution.py:43
  98.1 27.5 %collective-permute-start.14 = (bf16[2,2,128,768]{3,2,1,0:T(8,128)(2,1)}, bf16[2,2,128,768]{3,2,1,0:T(8,128)(2,1)}, u32[]{:S(2)}, u32[]{:S(2)}) collective-permute-start(bf16[2,2,128,768]{3,2,1,0:T(8,128)(2,1)} %copy-done.9), channel_id=1, source_target_pairs={{0,8},{8,0},{16,24},{24,16},{1,9},{9,1},{17,25},{25,17},{2,10},{10... | collective-permute-start | bytes 2359304 | tf_op jit(solution)/shard_map/ppermute | solution.py:43
  101.2 14.7 %collective-permute-start.43 = (bf16[2,96,768]{2,1,0:T(8,128)(2,1)}, bf16[2,96,768]{2,1,0:T(8,128)(2,1)S(1)}, u32[]{:S(2)}, u32[]{:S(2)}) collective-permute-start(bf16[2,96,768]{2,1,0:T(8,128)(2,1)} %get-tuple-element.111), channel_id=1, source_target_pairs={{0,1},{1,0},{2,3},{3,2},{4,5},{5,4},{6,7},{7,6},{8,9},{9,8},{10,11... | collective-permute-start | bytes 884744 | tf_op jit(solution)/shard_map/ppermute | solution.py:43
  120.1 17.2 %collective-permute-start.46 = (bf16[96,768]{1,0:T(8,128)(2,1)S(1)}, bf16[96,768]{1,0:T(8,128)(2,1)S(1)}, u32[]{:S(2)}, u32[]{:S(2)}) collective-permute-start(bf16[96,768]{1,0:T(8,128)(2,1)S(1)} %get-tuple-element.115), channel_id=1, source_target_pairs={{0,4},{1,5},{2,6},{3,7},{4,0},{5,1},{6,2},{7,3},{8,12},{9,13},{10,... | collective-permute-start | bytes 442376 | tf_op jit(solution)/shard_map/ppermute | solution.py:43
  122.5 21.1 %collective-permute-start.22 = (bf16[2,48,768]{2,1,0:T(8,128)(2,1)S(1)}, bf16[2,48,768]{2,1,0:T(8,128)(2,1)S(1)}, u32[]{:S(2)}, u32[]{:S(2)}) collective-permute-start(bf16[2,48,768]{2,1,0:T(8,128)(2,1)S(1)} %get-tuple-element.93), channel_id=1, source_target_pairs={{0,4},{1,5},{2,6},{3,7},{4,0},{5,1},{6,2},{7,3},{8,12},{9,13},{10,... | collective-permute-start | bytes 442376 | tf_op jit(solution)/shard_map/ppermute | solution.py:43
  124.3 22.4 %collective-permute-start.38 = (bf16[2,48,768]{2,1,0:T(8,128)(2,1)S(1)}, bf16[2,48,768]{2,1,0:T(8,128)(2,1)S(1)}, u32[]{:S(2)}, u32[]{:S(2)}) collective-permute-start(bf16[2,48,768]{2,1,0:T(8,128)(2,1)S(1)} %get-tuple-element.109), channel_id=1, source_target_pairs={{0,4},{1,5},{2,6},{3,7},{4,0},{5,1},{6,2},{7,3},{8,12},{9,13},{10,... | collective-permute-start | bytes 442376 | tf_op jit(solution)/shard_map/ppermute | solution.py:43
  126.7 37.1 %collective-permute-start.15 = (bf16[2,128,768]{2,1,0:T(8,128)(2,1)S(1)}, bf16[2,128,768]{2,1,0:T(8,128)(2,1)S(1)}, u32[]{:S(2)}, u32[]{:S(2)}) collective-permute-start(bf16[2,128,768]{2,1,0:T(8,128)(2,1)S(1)} %shard_map.277), channel_id=1, source_target_pairs={{0,16},{8,24},{16,0},{24,8},{1,17},{9,25},{17,1},{25,9},{2,18},{10... | collective-permute-start | bytes 1179656 | tf_op jit(solution)/shard_map/ppermute | solution.py:43
  137.3 15.8 %collective-permute-start.47 = (bf16[96,768]{1,0:T(8,128)(2,1)S(1)}, bf16[96,768]{1,0:T(8,128)(2,1)S(1)}, u32[]{:S(2)}, u32[]{:S(2)}) collective-permute-start(bf16[96,768]{1,0:T(8,128)(2,1)S(1)} %shard_map.295.refs_0_), channel_id=1, source_target_pairs={{0,4},{1,5},{2,6},{3,7},{4,0},{5,1},{6,2},{7,3},{8,12},{9,13},{10,... | collective-permute-start | bytes 442376 | tf_op jit(solution)/shard_map/ppermute | solution.py:43
  143.6 15.9 %collective-permute-start.23 = (bf16[2,48,768]{2,1,0:T(8,128)(2,1)S(1)}, bf16[2,48,768]{2,1,0:T(8,128)(2,1)S(1)}, u32[]{:S(2)}, u32[]{:S(2)}) collective-permute-start(bf16[2,48,768]{2,1,0:T(8,128)(2,1)S(1)} %shard_map.281.refs_0_), channel_id=1, source_target_pairs={{0,4},{1,5},{2,6},{3,7},{4,0},{5,1},{6,2},{7,3},{8,12},{9,13},{10,... | collective-permute-start | bytes 442376 | tf_op jit(solution)/shard_map/ppermute | solution.py:43
  146.8 15.5 %collective-permute-start.39 = (bf16[2,48,768]{2,1,0:T(8,128)(2,1)S(1)}, bf16[2,48,768]{2,1,0:T(8,128)(2,1)S(1)}, u32[]{:S(2)}, u32[]{:S(2)}) collective-permute-start(bf16[2,48,768]{2,1,0:T(8,128)(2,1)S(1)} %shard_map.290.refs_0_), channel_id=1, source_target_pairs={{0,4},{1,5},{2,6},{3,7},{4,0},{5,1},{6,2},{7,3},{8,12},{9,13},{10,... | collective-permute-start | bytes 442376 | tf_op jit(solution)/shard_map/ppermute | solution.py:43
  162.2 24.1 %collective-permute-start.25 = (bf16[4,48,768]{2,1,0:T(8,128)(2,1)S(1)}, bf16[4,48,768]{2,1,0:T(8,128)(2,1)S(1)}, u32[]{:S(2)}, u32[]{:S(2)}) collective-permute-start(bf16[4,48,768]{2,1,0:T(8,128)(2,1)S(1)} %bitcast.67), channel_id=1, source_target_pairs={{0,1},{1,0},{2,3},{3,2},{4,5},{5,4},{6,7},{7,6},{8,9},{9,8},{10,11... | collective-permute-start | bytes 884744 | tf_op jit(solution)/shard_map/ppermute | solution.py:43
  163.8 14.6 %collective-permute-start.40 = (bf16[4,48,768]{2,1,0:T(8,128)(2,1)S(1)}, bf16[4,48,768]{2,1,0:T(8,128)(2,1)S(1)}, u32[]{:S(2)}, u32[]{:S(2)}) collective-permute-start(bf16[4,48,768]{2,1,0:T(8,128)(2,1)S(1)} %bitcast.63), channel_id=1, source_target_pairs={{0,1},{1,0},{2,3},{3,2},{4,5},{5,4},{6,7},{7,6},{8,9},{9,8},{10,11... | collective-permute-start | bytes 884744 | tf_op jit(solution)/shard_map/ppermute | solution.py:43
  167.7 24.3 %collective-permute-start.41 = (bf16[4,48,768]{2,1,0:T(8,128)(2,1)S(1)}, bf16[4,48,768]{2,1,0:T(8,128)(2,1)S(1)}, u32[]{:S(2)}, u32[]{:S(2)}) collective-permute-start(bf16[4,48,768]{2,1,0:T(8,128)(2,1)S(1)} %bitcast.64), channel_id=1, source_target_pairs={{0,2},{1,3},{2,0},{3,1},{4,6},{5,7},{6,4},{7,5},{8,10},{9,11},{10,... | collective-permute-start | bytes 884744 | tf_op jit(solution)/shard_map/ppermute | solution.py:43
  167.7 17.0 %collective-permute-start.50 = (bf16[2,96,768]{2,1,0:T(8,128)(2,1)S(1)}, bf16[2,96,768]{2,1,0:T(8,128)(2,1)S(1)}, u32[]{:S(2)}, u32[]{:S(2)}) collective-permute-start(bf16[2,96,768]{2,1,0:T(8,128)(2,1)S(1)} %collective-permute-done.48.refs_1_), channel_id=1, source_target_pairs={{0,1},{1,0},{2,3},{3,2},{4,5},{5,4},{6,7},{7,6},{8,9},{9,8},{10,11... | collective-permute-start | bytes 884744 | tf_op jit(solution)/shard_map/ppermute | solution.py:43
  174.1 16.2 %collective-permute-start.26 = (bf16[4,48,768]{2,1,0:T(8,128)(2,1)S(1)}, bf16[4,48,768]{2,1,0:T(8,128)(2,1)S(1)}, u32[]{:S(2)}, u32[]{:S(2)}) collective-permute-start(bf16[4,48,768]{2,1,0:T(8,128)(2,1)S(1)} %collective-permute-done.24.refs_1_), channel_id=1, source_target_pairs={{0,1},{1,0},{2,3},{3,2},{4,5},{5,4},{6,7},{7,6},{8,9},{9,8},{10,11... | collective-permute-start | bytes 884744 | tf_op jit(solution)/shard_map/ppermute | solution.py:43
  (57 other events, 515.5 us)
where the time goes:
time: 195 us; the launch traced here: 194 us
  waiting for transfers between devices  68.8 us (35%)
  starting transfers between devices  49.3 us (25%)
  Pallas kernels  31.6 us (16%)
  local copies, waits for them, and re-layouts  27.3 us (14%)
  between operations  9.07 us (5%)
  other arithmetic  8.08 us (4%)
    ppermute x51, waiting for transfers between devices, swap(): return lax.ppermute(value, axis, [(i, i ^ bit) for i in range(size)])  68.8 us
    ppermute x51, starting transfers between devices, swap(): return lax.ppermute(value, axis, [(i, i ^ bit) for i in range(size)])  49.3 us
    pallas_call x26, Pallas kernels, call(): pl.pallas_call(kernel, out_shape=shapes, scratch_shapes=[pltpu.VMEM(s, d)...  31.6 us
    unnamed x61, local copies, waits for them, and re-layouts  9.97 us
    concatenate x1, local copies, waits for them, and re-layouts, body(): jnp.concatenate([ln1_gain, ln1_bias, ln2_gain, ln2_bias, b_out, b_down, b...  4.77 us
  transfers between devices with their start and end apart: 51, of which 20 were waited for; matrix products, arithmetic and copies ran while one was open for 13% of the time, Pallas kernels for 9%

commit v1 on v0

v1 whole, which is shorter than its diff:
```python
import math

import jax
import jax.numpy as jnp
from jax import lax
from jax.experimental import pallas as pl
from jax.experimental.pallas import tpu as pltpu
from jax.sharding import PartitionSpec as P


HEAD_DIM = 64
ROT = 16

EPSILON = 1e-05
INV_ROOT_TWO = 0.7071067811865476
INV_ROOT_TWO_PI = 0.3989422804014327


BF = jnp.bfloat16
F32 = jnp.float32


def as_float(array_in):
    return array_in.astype(F32)


def dot(left, right, dims):
    return lax.dot_general(left, right, (dims, ((), ())), preferred_element_type=F32)


def normalize(values):
    centre = values - jnp.mean(values, axis=-1, keepdims=True)
    inv_std = lax.rsqrt(jnp.mean(centre * centre, axis=-1, keepdims=True) + EPSILON)
    return (centre * inv_std, inv_std)


def gelu_parts(pre_act):
    cdf = 0.5 * (1.0 + lax.erf(pre_act * INV_ROOT_TWO))
    return pre_act * cdf, cdf + pre_act * jnp.exp(-0.5 * pre_act * pre_act) * INV_ROOT_TWO_PI


def swap(value, axis, size, bit):
    return lax.ppermute(value, axis, [(i, i ^ bit) for i in range(size)])


def powers(size):
    return [1 << k for k in range(size.bit_length() - 1)]


def call(kernel, outs, ins, scratch=(), flops=0, limit=8):
    shapes = [jax.ShapeDtypeStruct(s, d) for s, d in outs]
    moved = sum(math.prod(v.shape) * v.dtype.itemsize for v in [*ins, *shapes])
    return pl.pallas_call(
        kernel,
        out_shape=shapes,
        scratch_shapes=[pltpu.VMEM(s, d) for s, d in scratch],
        compiler_params=pltpu.CompilerParams(vmem_limit_bytes=limit * 1024 * 1024),
        cost_estimate=pl.CostEstimate(flops=flops, bytes_accessed=moved, transcendentals=0),
    )(*ins)


def bit_of(axis, bit):
    return jnp.where((lax.axis_index(axis) & bit) != 0, 1, 0).astype(jnp.int32)


def pack_kernel(wq, wu, pos, g1, b1, g2, b2, bo, bd, bq, q0, q1, q2, q3, u0, u1, u2, u3, small, scr):
    me = lax.axis_index("shard")
    rows = wq.shape[0]
    count = pos.shape[1]
    for k, ref in enumerate((g1, b1, g2, b2, bo, bd)):
        small[k : k + 1, :rows] = as_float(ref[...]).reshape(1, rows)
    small[6:7, : 3 * rows] = as_float(bq[...]).reshape(1, 3 * rows)
    small[7:8, :count] = as_float(pos[...])
    width = wq.shape[1] // 3
    wide = u0.shape[1]
    n_h = rows // HEAD_DIM
    for t in range(4):
        base = rows * t
        for h in range(n_h):
            a = base + HEAD_DIM * h
            scr[t, :, 2 * HEAD_DIM * h : 2 * HEAD_DIM * h + HEAD_DIM] = wq[:, a : a + HEAD_DIM]
            scr[t, :, 2 * HEAD_DIM * h + HEAD_DIM : 2 * HEAD_DIM * (h + 1)] = wq[
                :, width + a : width + a + HEAD_DIM
            ]
        scr[t, :, 2 * rows : 3 * rows] = wq[:, 2 * width + base : 2 * width + base + rows]
    for k, (q, u) in enumerate(((q0, u0), (q1, u1), (q2, u2), (q3, u3))):
        t = me ^ k
        q[...] = scr[t]
        u[...] = wu[:, pl.ds(pl.multiple_of(t * wide, 128), wide)]


def normed_of(ref):
    return normalize(ref[...].astype(F32))[0]


def write_rows(targets, grid, first, second, place):
    for target, half, b in zip(
        targets, (1 - first, 1 - first, first, first), (1 - second, second, 1 - second, second)
    ):
        n_t, n_r, _ = target.shape
        for t in range(n_t):
            start = pl.multiple_of(place(half, b, t), 16)
            target[t] = grid[pl.ds(start, n_r), :]


def prep_kernel(x0, x1, x2, x3, c0, c1, c2, c3, s0, s1, s2, s3, wd, wo,
                hid1, hid1_t, hid2, hid2_t, cot, dact, datt, csum, vec, bq_own, pos, sm, bq):
    me = lax.axis_index("shard")
    count = x0.shape[0]
    rows = wo.shape[0]
    width = wo.shape[1]
    for j, ref in enumerate((s0, s1, s2, s3)):
        sm[me ^ j] = ref[...]
    vec[...] = jnp.zeros_like(vec)
    for s in range(4):
        for k in range(6):
            vec[k : k + 1, rows * s : rows * (s + 1)] = sm[s, k : k + 1, :rows]
        bq[:, 3 * rows * s : 3 * rows * (s + 1)] = sm[s, 6:7, :]
        pos[:, count * s : count * (s + 1)] = sm[s, 7:8, :count]
    for t in range(4):

        @pl.when(me == t)
        def _(t=t):
            for part in range(3):
                for h in range(rows // HEAD_DIM):
                    a = part * width + rows * t + HEAD_DIM * h
                    b = HEAD_DIM * (2 * h + part) if part < 2 else 2 * rows + HEAD_DIM * h
                    bq_own[:, b : b + HEAD_DIM] = bq[:, a : a + HEAD_DIM]

    gain1, bias1, gain2, bias2 = (vec[k : k + 1, :] for k in range(4))
    for j, (x, c) in enumerate(((x0, c0), (x1, c1), (x2, c2), (x3, c3))):
        place = pl.ds(pl.multiple_of((me ^ j) * count, count), count)
        normed = normed_of(x)
        hid1[place, :] = (normed * gain1 + bias1).astype(BF)
        hid2[place, :] = (normed * gain2 + bias2).astype(BF)
        cot[place, :] = c[...]
    hid1_t[...] = hid1[...].T
    hid2_t[...] = hid2[...].T
    dact[...] = dot(cot[...], wd[...], ((1,), (1,)))
    datt[...] = dot(cot[...], wo[...], ((1,), (1,))).astype(BF)
    csum[...] = jnp.sum(as_float(cot[...]), axis=0, keepdims=True)


def att_kernel(order, hid, hid_t, cot, datt, q0, q1, q2, q3, bq, ca, sa, sb, segc, segr,
               sa_o, sb_o, ka_o, kb_o, att_o, dproj_o, wfull, bsum, neg, grid):
    me = lax.axis_index("shard")
    first, second = (bit_of("rep", bit) for bit in order)
    rows = q0.shape[0]
    length, width = cot.shape
    two = 2 * HEAD_DIM
    n_h = rows // HEAD_DIM
    for j, q in enumerate((q0, q1, q2, q3)):
        wfull[pl.ds(pl.multiple_of((me ^ j) * rows, 16), rows), :] = q[...]
    col = lax.broadcasted_iota(jnp.int32, (length, length), 1)
    row = lax.broadcasted_iota(jnp.int32, (length, length), 0)
    neg[...] = jnp.where((col <= row) & (segc[...] == segr[...]), 0.0, -jnp.inf)
    proj = dot(hid[...], wfull[...], ((1,), (0,))) + bq[...]
    for h in range(n_h):
        qk = proj[:, two * h : two * (h + 1)]
        qk = qk * ca[...] + pltpu.roll(qk, two - ROT // 2, 1) * sa[...] + pltpu.roll(qk, ROT // 2, 1) * sb[...]
        qk = qk.astype(BF)
        query, key = qk[:, :HEAD_DIM], qk[:, HEAD_DIM:]
        vals = slice(2 * rows + HEAD_DIM * h, 2 * rows + HEAD_DIM * (h + 1))
        val = proj[:, vals].astype(BF)
        da = datt[:, HEAD_DIM * h : HEAD_DIM * (h + 1)]
        scores = dot(query * jnp.asarray(0.125, BF), key, ((1,), (1,))) + neg[...]
        top = jnp.max(scores, axis=-1, keepdims=True)
        expo = jnp.exp(scores - top)
        prob = expo * (1.0 / jnp.sum(expo, axis=-1, keepdims=True))
        prob_b = prob.astype(BF)
        att = dot(prob_b, val, ((1,), (0,))).astype(BF)
        att_o[:, HEAD_DIM * h : HEAD_DIM * (h + 1)] = att
        d_val = dot(prob_b, da, ((0,), (0,)))
        d_prob = dot(da, val, ((1,), (1,)))
        row_dot = jnp.sum(as_float(da) * as_float(att), axis=-1, keepdims=True)
        d_score = (prob * (d_prob - row_dot)).astype(BF)
        dqk = 0.125 * jnp.concatenate(
            [dot(d_score, key, ((1,), (0,))), dot(d_score, query, ((0,), (0,)))], axis=1
        )
        dqk = dqk * ca[...] - pltpu.roll(dqk, two - ROT // 2, 1) * sa[...] - pltpu.roll(dqk, ROT // 2, 1) * sb[...]
        dproj_o[:, two * h : two * (h + 1)] = dqk.astype(BF)
        dproj_o[:, vals] = d_val.astype(BF)
        bsum[:, two * h : two * (h + 1)] = jnp.sum(dqk, axis=0, keepdims=True)
        bsum[:, vals] = jnp.sum(d_val, axis=0, keepdims=True)
    grid[:, : 3 * rows] = dot(hid_t[...], dproj_o[...], ((1,), (0,))).astype(BF)
    g_out = dot(att_o[...], cot[...], ((0,), (0,))).astype(BF)
    for t in range(width // rows):
        grid[rows * t : rows * (t + 1), 3 * rows :] = g_out[:, rows * t : rows * (t + 1)]
    n_r = sa_o.shape[1]
    write_rows(
        (sa_o, sb_o, ka_o, kb_o), grid, first, second, lambda half, b, t: t * rows + (2 * half + b) * n_r
    )


def mlp1_kernel(order, hid, cot, u0, u1, u2, u3, bup, sa_o, sb_o, ka_o, kb_o, activ, slope, wfull, grid):
    me = lax.axis_index("shard")
    first, second = (bit_of("rep", bit) for bit in order)
    rows = u0.shape[0]
    for j, u in enumerate((u0, u1, u2, u3)):
        wfull[pl.ds(pl.multiple_of((me ^ j) * rows, 16), rows), :] = u[...]
    block = hid.shape[0] // 4
    for j in range(4):
        part = slice(block * j, block * (j + 1))
        pre_act = dot(hid[part, :], wfull[...], ((1,), (0,))) + bup[...]
        act, slp = gelu_parts(pre_act)
        activ[part, :] = act.astype(BF)
        slope[part, :] = slp
    grid[...] = dot(activ[...], cot[...], ((0,), (0,))).astype(BF)
    n_t, n_r, _ = sa_o.shape
    write_rows(
        (sa_o, sb_o, ka_o, kb_o), grid, first, second, lambda half, b, t: ((half * 2 + b) * n_t + t) * n_r
    )


def mlp2_kernel(order, dact, hid_t, slope, sa_o, sb_o, ka_o, kb_o, dpre, bsum, grid):
    first, second = (bit_of("rep", bit) for bit in order)
    d_pre = dact[...] * slope[...]
    dpre[...] = d_pre.astype(BF)
    bsum[...] = jnp.sum(d_pre, axis=0, keepdims=True)
    grid[...] = dot(hid_t[...], dpre[...], ((1,), (0,))).astype(BF)
    n_r = sa_o.shape[1]
    rows = n_r * 4
    write_rows(
        (sa_o, sb_o, ka_o, kb_o), grid, first, second, lambda half, b, t: t * rows + (2 * half + b) * n_r
    )


def mlp3_kernel(x0, x1, x2, x3, att, activ, dproj, dpre, wo, wd, wq, wu, vec,
                bsum, csum, bup, send, keep, vecs):
    me = lax.axis_index("shard")
    count = x0.shape[0]
    total = [None] * 4
    for j, x in enumerate((x0, x1, x2, x3)):
        part = pl.ds(pl.multiple_of((me ^ j) * count, count), count)
        out = dot(att[part, :], wo[...], ((1,), (0,))) + dot(activ[part, :], wd[...], ((1,), (0,)))
        one = dot(dproj[part, :], wq[...], ((1,), (1,)))
        two = dot(dpre[part, :], wu[...], ((1,), (1,)))
        normed = normed_of(x)
        target = keep if j % 2 == 0 else send
        target[j // 2, :count, :] = out.astype(BF)
        target[j // 2, count : 2 * count, :] = (one * vec[0:1, :] + two * vec[2:3, :]).astype(BF)
        for k, value in enumerate((one * normed, one, two * normed, two)):
            piece = jnp.sum(value, axis=0, keepdims=True)
            total[k] = piece if total[k] is None else total[k] + piece
    rows, _ = wo.shape
    n_h = rows // HEAD_DIM
    vecs[...] = jnp.zeros_like(vecs)
    for t in range(4):
        for k in range(4):
            vecs[t, 0:1, rows * k : rows * (k + 1)] = total[k][:, rows * t : rows * (t + 1)]

        @pl.when(me == t)
        def _(t=t):
            for part in range(3):
                owner, slot = divmod(4 * part + t, 3)
                for h in range(n_h):
                    a = HEAD_DIM * (2 * h + part) if part < 2 else 2 * rows + HEAD_DIM * h
                    b = rows * slot + HEAD_DIM * h
                    vecs[owner, 1:2, b : b + HEAD_DIM] = bsum[:, a : a + HEAD_DIM]
            vecs[t, 1:2, 3 * rows : 4 * rows] = csum[:, rows * t : rows * (t + 1)]
            vecs[t, 2:3, :] = bup[...]

    for j in range(4):
        target = keep if j % 2 == 0 else send
        target[j // 2, 2 * count :, :] = vecs[me ^ j].astype(BF)


def add_kernel(kept, got, out):
    out[...] = (as_float(kept[...]) + as_float(got[...])).astype(out.dtype)


def add_one_kernel(kept, got, out):
    out[...] = (as_float(kept[1]) + as_float(got[1])).astype(BF)


def add_split_kernel(bit, kept, got, more, send, keep):
    mine = bit_of("rep", bit)
    for place, out in ((1 - mine, send), (mine, keep)):
        out[...] = (as_float(kept[place]) + as_float(got[place]) + as_float(more[place])).astype(BF)


def add_pieces_kernel(kept, got, more, p0, p1, p2, p3, *rest):
    me = lax.axis_index("shard")
    cols = p0.shape[1]
    for k, p in enumerate((p0, p1, p2, p3)):
        t = me ^ k
        total = (as_float(kept[t]) + as_float(got[t]) + as_float(more[t])).astype(BF)
        p[...] = total[:, :cols]
        if rest:
            rest[0][t] = total[:, cols:]


def pieces_split_kernel(bit, p0, p1, p2, p3, *rest):
    me = lax.axis_index("shard")
    mine = bit_of("rep", bit)
    send, keep = rest[-2:]
    cols = p0.shape[1]
    for k, p in enumerate((p0, p1, p2, p3)):
        s = me ^ k
        pair, slot = s >> 1, s & 1
        for target, wanted in ((keep, mine), (send, 1 - mine)):

            @pl.when(pair == wanted)
            def _(target=target):
                target[slot, :, :cols] = p[...]
                if len(rest) > 2:
                    target[slot, :, cols:] = rest[0][s]


def last_kernel(kept, got, vec, out):
    n, n_r, _ = kept.shape
    for k in range(n):
        out[n_r * k : n_r * (k + 1), :] = (as_float(kept[k]) + as_float(got[k])).astype(BF)
    out[n_r * n :, :] = vec[...]


def pair_vec_kernel(bit, own, got, out):
    mine = bit_of("rep", bit)
    n = (out.shape[0] - own.shape[0])
    out[pl.ds(pl.multiple_of(mine * n, 16), n), :] = own[:n, :]
    out[pl.ds(pl.multiple_of((1 - mine) * n, 16), n), :] = got[:n, :]
    out[2 * n :, :] = (as_float(own[n:, :]) + as_float(got[n:, :])).astype(BF)


def pair_kernel(bit, own, got, out):
    mine = bit_of("rep", bit)
    out[mine] = own[...]
    out[1 - mine] = got[...]


def quarters(order, refs):
    first, second = (bit_of("rep", bit) for bit in order)
    return zip(refs, (first, first, 1 - first, 1 - first), (second, 1 - second, second, 1 - second))


def final_down_kernel(order, p0, p1, p2, p3, out):
    for value, half, b in quarters(order, (p0, p1, p2, p3)):
        n_t, n_r, _ = value.shape
        for t in range(n_t):
            start = pl.multiple_of(((half * 2 + b) * n_t + t) * n_r, 8)
            out[pl.ds(start, n_r), :] = as_float(value[t])


def final_up_kernel(order, p0, p1, p2, p3, out, vec):
    n_r = out.shape[0] // 4
    wide = out.shape[1] // 4
    v0, v1, v2, v3 = (as_float(p[4 * n_r :, :]) for p in (p0, p1, p2, p3))
    vec[...] = (v0 + v1) + (v2 + v3)
    for value, half, b in quarters(order, (p0, p1, p2, p3)):
        start = pl.multiple_of((half * 2 + b) * n_r, 8)
        for s in range(4):
            out[pl.ds(start, n_r), wide * s : wide * (s + 1)] = as_float(value[n_r * s : n_r * (s + 1), :])


def final_qkv_kernel(order, p0, p1, p2, p3, out, out_w):
    rows = out_w.shape[0]
    n_h = rows // HEAD_DIM
    for value, half, b in quarters(order, (p0, p1, p2, p3)):
        n_s, n_r, width = value.shape
        place = pl.ds(pl.multiple_of((half * 2 + b) * n_r, 8), n_r)
        for s in range(n_s):
            block = as_float(value[s])
            for h in range(n_h):
                a = rows * s + HEAD_DIM * h
                two = 2 * HEAD_DIM * h
                out[place, a : a + HEAD_DIM] = block[:, two : two + HEAD_DIM]
                out[place, width + a : width + a + HEAD_DIM] = block[:, two + HEAD_DIM : two + 2 * HEAD_DIM]
            out[place, 2 * width + rows * s : 2 * width + rows * (s + 1)] = block[:, 2 * rows : 3 * rows]
            out_w[place, rows * s : rows * (s + 1)] = block[:, 3 * rows :]


def make_body(shards, reps):
    def body(
        block_input,
        positions,
        segments,
        w_qkv,
        b_qkv,
        w_out,
        b_out,
        w_up,
        b_up,
        w_down,
        b_down,
        ln1_gain,
        ln1_bias,
        ln2_gain,
        ln2_bias,
        cotangent,
    ):
        tokens_in = block_input[0]
        cotan_own = cotangent[0]
        count, width = tokens_in.shape
        length = segments.shape[1]
        rows = w_qkv.shape[0]
        wide = w_up.shape[1] // shards
        bits = powers(reps)

        def to(j, value):
            return swap(value, "shard", shards, j)

        def gather(value):
            two = to(2, value)
            one = to(1, value)
            return value, one, two, swap(two, "shard", shards, 1)

        x = gather(tokens_in)
        packed = call(
            pack_kernel,
            [((rows, 3 * rows), BF)] * 4 + [((rows, wide), BF)] * 4 + [((8, 3 * rows), F32)],
            (w_qkv, w_up, positions, ln1_gain, ln1_bias, ln2_gain, ln2_bias, b_out, b_down, b_qkv),
            scratch=[((4, rows, 3 * rows), BF)],
            limit=62,
        )
        q_w = (packed[0], *(to(j, packed[j]) for j in (1, 2, 3)))
        c = gather(cotan_own)
        u_w = (packed[4], *(to(j, packed[4 + j]) for j in (1, 2, 3)))

        small = gather(packed[8])
        first, second, third = bits[:3]
        order_att, order_down, order_up = (first, second), (first, second), (second, first)
        sub = rows // 4
        n_c = width // rows

        hid1, hid1_t, hid2, hid2_t, cot, dact, datt, csum, vec_in, bias_qkv, position_all = call(
            prep_kernel,
            [((length, width), BF), ((width, length), BF)] * 2
            + [((length, width), BF), ((length, wide), F32), ((length, rows), BF), ((1, width), F32)]
            + [((8, width), F32), ((1, 3 * rows), F32), ((1, length), F32)],
            (*x, *c, *small, w_down, w_out),
            scratch=[((4, 8, 3 * rows), F32), ((1, 3 * width), F32)],
            flops=1_000_000_000,
            limit=24,
        )
        half = ROT // 2
        lane = jnp.arange(2 * HEAD_DIM) % HEAD_DIM
        freqs = jnp.exp((lane % half).astype(F32) * (-math.log(10000.0) / half))
        angles = position_all.reshape(-1, 1) * freqs[None, :]
        cosine, sine = jnp.cos(angles), jnp.sin(angles)
        ca = jnp.where(lane < ROT, cosine, 1.0)
        sa = jnp.where(lane < half, -sine, 0.0)
        sb = jnp.where((lane >= half) & (lane < ROT), sine, 0.0)

        *grad_a, activ, slope, wu_full = call(
            lambda *refs: mlp1_kernel(order_down, *refs),
            [((2, wide // 8, width), BF)] * 4
            + [((length, wide), BF), ((length, wide), F32), ((width, wide), BF)],
            (hid2, cot, *u_w, as_float(b_up).reshape(1, -1)),
            scratch=[((wide, width), BF)],
            flops=2_000_000_000,
            limit=24,
        )
        *grad_b, dpre, bup_sum = call(
            lambda *refs: mlp2_kernel(order_up, *refs),
            [((shards, sub, wide), BF)] * 4 + [((length, wide), BF), ((1, wide), F32)],
            (dact, hid2_t, slope),
            scratch=[((width, wide), BF)],
            flops=2_000_000_000,
            limit=24,
        )
        *grad_c, att, dproj, wq_full, bsum = call(
            lambda *refs: att_kernel(order_att, *refs),
            [((n_c, sub, width), BF)] * 4
            + [
                ((length, rows), BF),
                ((length, 3 * rows), BF),
                ((width, 3 * rows), BF),
                ((1, 3 * rows), F32),
            ],
            (hid1, hid1_t, cot, datt, *q_w, bias_qkv, ca, sa, sb, segments.reshape(-1, 1), segments),
            scratch=[((length, length), F32), ((width, width), BF)],
            flops=4_000_000_000,
            limit=24,
        )
        rs_send, rs_keep = call(
            mlp3_kernel,
            [((2, 2 * count + 16, width), BF)] * 2,
            (*x, att, activ, dproj, dpre, w_out, w_down, wq_full, wu_full, vec_in,
             bsum, csum, bup_sum),
            scratch=[((4, 16, width), F32)],
            flops=3_000_000_000,
            limit=24,
        )

        def over(bit, value):
            return swap(value, "rep", reps, bit)

        got = to(1, rs_send)
        (onward,) = call(add_one_kernel, [(got.shape[1:], BF)], (rs_keep, got))
        total = as_float(rs_keep[0]) + as_float(got[0]) + as_float(to(2, onward))
        output = as_float(tokens_in) + total[:count] + vec_in[4:5] + vec_in[5:6]
        d_norm = total[count : 2 * count]
        vec_own = total[2 * count :].astype(BF)
        own_normed, inv_std = normalize(as_float(tokens_in))
        d_input = as_float(cotan_own) + inv_std * (
            d_norm
            - jnp.mean(d_norm, axis=-1, keepdims=True)
            - own_normed * jnp.mean(d_norm * own_normed, axis=-1, keepdims=True)
        )

        def start_sum(bit_order, grad):
            sent_a, sent_b, kept_a, kept_b = grad
            one, two = bit_order
            got_a = over(one, sent_a)
            got_b = over(one, sent_b)
            (sent,) = call(add_kernel, [(kept_a.shape, BF)], (kept_a, got_a))
            return kept_b, got_b, over(two, sent)

        def finish_sum(bit_order, sent, kept, shape, vec=None):
            one, two = bit_order
            got = over(third, sent)
            if vec is None:
                (own,) = call(add_kernel, [(kept.shape, BF)], (kept, got))
            else:
                n_rows = kept.shape[0] * kept.shape[1]
                shape = (2 * n_rows + vec.shape[0], shape[2])
                (own,) = call(last_kernel, [((n_rows + vec.shape[0], shape[1]), BF)], (kept, got, vec))
            for bit in bits[3:]:
                more = over(bit, own)
                (own,) = call(add_kernel, [(own.shape, BF)], (own, more))
            (both,) = call(
                lambda *refs: (pair_kernel if vec is None else pair_vec_kernel)(third, *refs),
                [((2, *own.shape) if vec is None else shape, BF)],
                (own, over(third, own)),
            )
            both = both.reshape(shape)
            other = over(two, both)
            return both, other, over(one, both), over(one, other)

        def shard_stream(bit_order, grad, cols, vec=None):
            held = start_sum(bit_order, grad)
            shape = held[0].shape
            extra = [] if cols == shape[2] else [((n_c, sub, shape[2] - cols), BF)]
            parts = call(add_pieces_kernel, [((sub, cols), BF)] * 4 + extra, held)
            mixed = (parts[0], *(to(j, parts[j]) for j in range(1, 4)), *parts[4:])
            sent, kept = call(lambda *refs: pieces_split_kernel(third, *refs), [((2, sub, shape[2]), BF)] * 2, mixed)
            return finish_sum(bit_order, sent, kept, shape, vec)

        def plain_stream(bit_order, grad):
            held = start_sum(bit_order, grad)
            shape = held[0].shape
            sent, kept = call(lambda *refs: add_split_kernel(third, *refs), [(shape[1:], BF)] * 2, held)
            return finish_sum(bit_order, sent, kept, shape)

        own_c = shard_stream(order_att, grad_c, 3 * rows)
        own_a = plain_stream(order_down, grad_a)
        own_b = shard_stream(order_up, grad_b, wide, vec_own)
        tot_qkv, tot_out = call(
            lambda *refs: final_qkv_kernel(order_att, *refs), [((rows, 3 * width), F32), ((rows, width), F32)], own_c
        )
        (tot_down,) = call(lambda *refs: final_down_kernel(order_down, *refs), [((wide, width), F32)], own_a)
        tot_up, vec = call(
            lambda *refs: final_up_kernel(order_up, *refs), [((rows, shards * wide), F32), (vec_own.shape, F32)], own_b
        )

        g1, bb1, g2, bb2 = [vec[0, k * rows : (k + 1) * rows] for k in range(4)]
        tot_bqkv = vec[1, : 3 * rows]
        tot_cot = vec[1, 3 * rows :]
        tot_bup = vec[2]
        return (
            output[None],
            d_input[None],
            tot_qkv,
            tot_bqkv,
            tot_out,
            tot_cot,
            tot_up,
            tot_bup,
            tot_down,
            tot_cot,
            g1,
            bb1,
            g2,
            bb2,
        )

    return body


def solution(mesh):
    body = make_body(mesh.shape["shard"], mesh.shape["rep"])
    return jax.shard_map(
        body,
        mesh=mesh,
        in_specs=(
            P("rep", "shard", None),
            P("rep", "shard"),
            P("rep", None),
            P("shard", None),
            P("shard"),
            P("shard", None),
            P("shard"),
            P("shard", None),
            P("shard"),
            P("shard", None),
            P("shard"),
            P("shard"),
            P("shard"),
            P("shard"),
            P("shard"),
            P("rep", "shard", None),
        ),
        out_specs=(
            P("rep", "shard", None),
            P("rep", "shard", None),
            P("shard", None),
            P("shard"),
            P("shard", None),
            P("shard"),
            P("shard", None),
            P("shard"),
            P("shard", None),
            P("shard"),
            P("shard"),
            P("shard"),
            P("shard"),
            P("shard"),
        ),
        check_vma=False,
    )
```

time: 195 us -> 171 us (0.88)
  local copies, waits for them, and re-layouts: 27.3 us -> 3.35 us
  starting transfers between devices: 49.3 us -> 62.2 us
  between operations: 9.07 us -> 1 us
  other arithmetic: 8.08 us -> 2.73 us
  waiting for transfers between devices: 68.8 us -> 72.9 us
  Pallas kernels: 31.6 us -> 27.8 us
    ppermute x51 -> x47, starting transfers between devices: 49.3 us -> 62.2 us  [swap(): return lax.ppermute(value, axis, [(i, i ^ bit) for i in range(size)])]
    unnamed x61 -> x23, local copies, waits for them, and re-layouts: 9.97 us -> 1.33 us
    concatenate x4 -> x0, local copies, waits for them, and re-layouts: 5.73 us -> none  [the longest x1 4.77 us: body(): jnp.concatenate([ln1_gain, ln1_bias, ln2_gain, ln2_bias, b_out, b_down, b...]
    ppermute x51 -> x47, waiting for transfers between devices: 68.8 us -> 72.9 us  [swap(): return lax.ppermute(value, axis, [(i, i ^ bit) for i in range(size)])]
    pallas_call x26 -> x24, Pallas kernels: 31.6 us -> 27.8 us  [call(): pl.pallas_call(kernel, out_shape=shapes, scratch_shapes=[pltpu.VMEM(s, d)...]
    add x10 -> x0, other arithmetic: 3.15 us -> none  [the longest x2 1.35 us: cube_scatter(): value = value[:half] + swap(value[half:], axis, size, bit)]
    convert_element_type x6 -> x0, local copies, waits for them, and re-layouts: 2.45 us -> none  [as_float(): return array_in.astype(F32)]
  transfers between devices with their start and end apart: 51 -> 47, of which waited for: 20 -> 21; matrix products, arithmetic and copies ran while one was open for 13% -> 2% of each run, Pallas kernels for 9% -> 8%
where the time goes in v1:
time: 171 us; the launch traced here: 170 us
  waiting for transfers between devices  72.9 us (43%)
  starting transfers between devices  62.2 us (36%)
  Pallas kernels  27.8 us (16%)
  local copies, waits for them, and re-layouts  3.35 us (2%)
  other arithmetic  2.73 us (2%)
    ppermute x47, waiting for transfers between devices, swap(): return lax.ppermute(value, axis, [(i, i ^ bit) for i in range(size)])  72.9 us
    ppermute x47, starting transfers between devices, swap(): return lax.ppermute(value, axis, [(i, i ^ bit) for i in range(size)])  62.2 us
    pallas_call x24, Pallas kernels, call(): pl.pallas_call(kernel, out_shape=shapes, scratch_shapes=[pltpu.VMEM(s, d)...  27.8 us
  transfers between devices with their start and end apart: 47, of which 21 were waited for; matrix products, arithmetic and copies ran while one was open for 2% of the time, Pallas kernels for 8%

profile of v1, /device:TPU:0, one launch (start us, length us, event | category | flops | bytes accessed | tf_op | source)
XLA Modules:
  0.0 169.9 jit_solution(3425941576369499167)
XLA Ops:
  1.3 2.6 %collective-permute-start.1 = (bf16[128,768]{1,0:T(8,128)(2,1)}, bf16[128,768]{1,0:T(8,128)(2,1)}, u32[]{:S(2)}, u32[]{:S(2)}) collective-permute-start(bf16[128,768]{1,0:T(8,128)(2,1)} %bitcast.23), channel_id=1, source_target_pairs={{0,16},{8,24},{16,0},{24,8},{1,17},{9,25},{17,1},{25,9},{2,18},{10... | collective-permute-start | bytes 589832 | tf_op jit(solution)/shard_map/ppermute | solution.py:43
  4.3 3.3 %shard_map.263 = (bf16[192,576]{1,0:T(8,128)(2,1)}, bf16[192,576]{1,0:T(8,128)(2,1)}, bf16[192,576]{1,0:T(8,128)(2,1)}, bf16[192,576]{1,0:T(8,128)(2,1)}, bf16[1...) custom-call(bf16[192,2304]{1,0:T(8,128)(2,1)} %wq.1, ...), custom_call_target="tpu_custom_call" | custom-call | bytes 4151168 | tf_op jit(solution)/shard_map/pallas_call | solution.py:53
  10.7 3.4 %collective-permute-done.7.s2 = f32[8,576]{1,0:T(8,128)S(1)} collective-permute-done((f32[8,576]{1,0:T(8,128)}, f32[8,576]{1,0:T(8,128)S(1)}, u32[]{:S(2)}, u32[]{:S(2)}) %collective-permute-start.7) | collective-permute-done | bytes 18464 | tf_op jit(solution)/shard_map/ppermute | solution.py:43
  21.8 3.1 %shard_map.264 = (bf16[512,768]{1,0:T(8,128)(2,1)S(1)}, bf16[768,512]{1,0:T(8,128)(2,1)S(1)}, bf16[512,768]{1,0:T(8,128)(2,1)S(1)}, bf16[768,512]{1,0:T(8,128)(2...) custom-call(bf16[128,768]{1,0:T(8,128)(2,1)S(1)} %bitcast.24, ...), custom_call_target="tpu_custom_call" | custom-call | flops 1000000000 | bytes 8854784 | tf_op jit(solution)/shard_map/pallas_call | solution.py:53
  25.6 5.7 %collective-permute-done.14.refs_5_ = bf16[192,768]{1,0:T(8,128)(2,1)S(1)} collective-permute-done((bf16[192,768]{1,0:T(8,128)(2,1)}, bf16[192,768]{1,0:T(8,128)(2,1)S(1)}, u32[]{:S(2)}, u32[]{:S(2)}) %collective-permute-start.14) | collective-permute-done | bytes 294944 | tf_op jit(solution)/shard_map/ppermute | solution.py:43
  37.2 4.0 %collective-permute-done.11.refs_7_ = bf16[192,576]{1,0:T(8,128)(2,1)S(1)} collective-permute-done((bf16[192,576]{1,0:T(8,128)(2,1)S(1)}, bf16[192,576]{1,0:T(8,128)(2,1)S(1)}, u32[]{:S(2)}, u32[]{:S(2)}) %collective-permute-start.11) | collective-permute-done | bytes 221216 | tf_op jit(solution)/shard_map/ppermute | solution.py:43
  41.2 7.0 %shard_map.265 = (bf16[4,48,768]{2,1,0:T(8,128)(2,1)S(1)}, bf16[4,48,768]{2,1,0:T(8,128)(2,1)S(1)}, bf16[4,48,768]{2,1,0:T(8,128)(2,1)S(1)}, bf16[4,48,768]{2,1,...) custom-call(bf16[512,768]{1,0:T(8,128)(2,1)S(1)} %get-tuple-element., ...), custom_call_target="tpu_custom_call" | custom-call | flops 4000000000 | bytes 7086592 | tf_op jit(solution)/shard_map/pallas_call | solution.py:53
  48.2 5.2 %shard_map.268 = (bf16[2,272,768]{2,1,0:T(8,128)(2,1)S(1)}, bf16[2,272,768]{2,1,0:T(8,128)(2,1)S(1)}) custom-call(bf16[128,768]{1,0:T(8,128)(2,1)S(1)} %bitcast.25, bf16[128,768]{1,0:T(8,128)(2,1)} %collective-permute-done.x1, bf16[128,768]{1,0:T(8,128)(2,1)} %collective-permute-done.1.x2, bf16[128,768]{1,0:T(8,128)(2,1)S(1)} %collective-permute-done.2.x3, ...), custom_call_target="tpu_custom_call" | custom-call | flops 3000000000 | bytes 8388864 | tf_op jit(solution)/shard_map/pallas_call | solution.py:53
  59.3 4.5 %collective-permute-done.18.got = bf16[4,48,768]{2,1,0:T(8,128)(2,1)S(1)} collective-permute-done((bf16[4,48,768]{2,1,0:T(8,128)(2,1)S(1)}, bf16[4,48,768]{2,1,0:T(8,128)(2,1)S(1)}, u32[]{:S(2)}, u32[]{:S(2)}) %collective-permute-start.18) | collective-permute-done | bytes 294944 | tf_op jit(solution)/shard_map/ppermute | solution.py:43
  65.7 4.4 %collective-permute-done.40.got = bf16[2,96,768]{2,1,0:T(8,128)(2,1)S(1)} collective-permute-done((bf16[2,96,768]{2,1,0:T(8,128)(2,1)S(1)}, bf16[2,96,768]{2,1,0:T(8,128)(2,1)S(1)}, u32[]{:S(2)}, u32[]{:S(2)}) %collective-permute-start.40) | collective-permute-done | bytes 294944 | tf_op jit(solution)/shard_map/ppermute | solution.py:43
  73.7 2.8 %collective-permute-done.17.got = bf16[4,48,768]{2,1,0:T(8,128)(2,1)S(1)} collective-permute-done((bf16[4,48,768]{2,1,0:T(8,128)(2,1)S(1)}, bf16[4,48,768]{2,1,0:T(8,128)(2,1)S(1)}, u32[]{:S(2)}, u32[]{:S(2)}) %collective-permute-start.17) | collective-permute-done | bytes 294944 | tf_op jit(solution)/shard_map/ppermute | solution.py:43
  79.9 2.8 %collective-permute-done.39.refs_1_ = bf16[2,96,768]{2,1,0:T(8,128)(2,1)S(1)} collective-permute-done((bf16[2,96,768]{2,1,0:T(8,128)(2,1)S(1)}, bf16[2,96,768]{2,1,0:T(8,128)(2,1)S(1)}, u32[]{:S(2)}, u32[]{:S(2)}) %collective-permute-start.39) | collective-permute-done | bytes 294944 | tf_op jit(solution)/shard_map/ppermute | solution.py:43
  87.2 2.8 %collective-permute-start.42 = (bf16[96,768]{1,0:T(8,128)(2,1)S(1)}, bf16[96,768]{1,0:T(8,128)(2,1)S(1)}, u32[]{:S(2)}, u32[]{:S(2)}) collective-permute-start(bf16[96,768]{1,0:T(8,128)(2,1)S(1)} %get-tuple-element.137), channel_id=1, source_target_pairs={{0,4},{1,5},{2,6},{3,7},{4,0},{5,1},{6,2},{7,3},{8,12},{9,13},{10,... | collective-permute-start | bytes 442376 | tf_op jit(solution)/shard_map/ppermute | solution.py:43
  93.4 7.7 %collective-permute-done.42.got = bf16[96,768]{1,0:T(8,128)(2,1)S(1)} collective-permute-done((bf16[96,768]{1,0:T(8,128)(2,1)S(1)}, bf16[96,768]{1,0:T(8,128)(2,1)S(1)}, u32[]{:S(2)}, u32[]{:S(2)}) %collective-permute-start.42) | collective-permute-done | bytes 147488 | tf_op jit(solution)/shard_map/ppermute | solution.py:43
  101.2 2.5 %collective-permute-done.23.got = bf16[2,48,768]{2,1,0:T(8,128)(2,1)S(1)} collective-permute-done((bf16[2,48,768]{2,1,0:T(8,128)(2,1)S(1)}, bf16[2,48,768]{2,1,0:T(8,128)(2,1)S(1)}, u32[]{:S(2)}, u32[]{:S(2)}) %collective-permute-start.23) | collective-permute-done | bytes 147488 | tf_op jit(solution)/shard_map/ppermute | solution.py:43
  106.0 2.6 %collective-permute-done.32.refs_2_ = bf16[48,768]{1,0:T(8,128)(2,1)S(1)} collective-permute-done((bf16[48,768]{1,0:T(8,128)(2,1)S(1)}, bf16[48,768]{1,0:T(8,128)(2,1)S(1)}, u32[]{:S(2)}, u32[]{:S(2)}) %collective-permute-start.32) | collective-permute-done | bytes 73760 | tf_op jit(solution)/shard_map/ppermute | solution.py:43
  110.2 2.6 %collective-permute-start.34 = (bf16[2,48,768]{2,1,0:T(8,128)(2,1)S(1)}, bf16[2,48,768]{2,1,0:T(8,128)(2,1)S(1)}, u32[]{:S(2)}, u32[]{:S(2)}) collective-permute-start(bf16[2,48,768]{2,1,0:T(8,128)(2,1)S(1)} %get-tuple-element.128), channel_id=1, source_target_pairs={{0,4},{1,5},{2,6},{3,7},{4,0},{5,1},{6,2},{7,3},{8,12},{9,13},{10,... | collective-permute-start | bytes 442376 | tf_op jit(solution)/shard_map/ppermute | solution.py:43
  112.8 7.2 %collective-permute-start.44 = (bf16[2,96,768]{2,1,0:T(8,128)(2,1)S(1)}, bf16[2,96,768]{2,1,0:T(8,128)(2,1)S(1)}, u32[]{:S(2)}, u32[]{:S(2)}) collective-permute-start(bf16[2,96,768]{2,1,0:T(8,128)(2,1)S(1)} %shard_map.285.refs_0_), channel_id=1, source_target_pairs={{0,2},{1,3},{2,0},{3,1},{4,6},{5,7},{6,4},{7,5},{8,10},{9,11},{10,... | collective-permute-start | bytes 884744 | tf_op jit(solution)/shard_map/ppermute | solution.py:43
  120.5 3.4 %collective-permute-start.35 = (bf16[112,768]{1,0:T(8,128)(2,1)S(1)}, bf16[112,768]{1,0:T(8,128)(2,1)S(1)}, u32[]{:S(2)}, u32[]{:S(2)}) collective-permute-start(bf16[112,768]{1,0:T(8,128)(2,1)S(1)} %shard_map.279.refs_0_), channel_id=1, source_target_pairs={{0,4},{1,5},{2,6},{3,7},{4,0},{5,1},{6,2},{7,3},{8,12},{9,13},{10,... | collective-permute-start | bytes 516104 | tf_op jit(solution)/shard_map/ppermute | solution.py:43
  126.1 5.5 %collective-permute-done.44.refs_1_ = bf16[2,96,768]{2,1,0:T(8,128)(2,1)S(1)} collective-permute-done((bf16[2,96,768]{2,1,0:T(8,128)(2,1)S(1)}, bf16[2,96,768]{2,1,0:T(8,128)(2,1)S(1)}, u32[]{:S(2)}, u32[]{:S(2)}) %collective-permute-start.44) | collective-permute-done | bytes 294944 | tf_op jit(solution)/shard_map/ppermute | solution.py:43
  133.1 4.1 %collective-permute-done.25.refs_1_ = bf16[4,48,768]{2,1,0:T(8,128)(2,1)S(1)} collective-permute-done((bf16[4,48,768]{2,1,0:T(8,128)(2,1)S(1)}, bf16[4,48,768]{2,1,0:T(8,128)(2,1)S(1)}, u32[]{:S(2)}, u32[]{:S(2)}) %collective-permute-start.25) | collective-permute-done | bytes 294944 | tf_op jit(solution)/shard_map/ppermute | solution.py:43
  139.5 5.2 %collective-permute-start.37 = (bf16[208,768]{1,0:T(8,128)(2,1)S(1)}, bf16[208,768]{1,0:T(8,128)(2,1)S(1)}, u32[]{:S(2)}, u32[]{:S(2)}) collective-permute-start(bf16[208,768]{1,0:T(8,128)(2,1)S(1)} %shard_map.280.refs_0_), channel_id=1, source_target_pairs={{0,2},{1,3},{2,0},{3,1},{4,6},{5,7},{6,4},{7,5},{8,10},{9,11},{10,... | collective-permute-start | bytes 958472 | tf_op jit(solution)/shard_map/ppermute | solution.py:43
  144.7 13.0 %collective-permute-done.36.refs_1_ = bf16[208,768]{1,0:T(8,128)(2,1)S(1)} collective-permute-done((bf16[208,768]{1,0:T(8,128)(2,1)S(1)}, bf16[208,768]{1,0:T(8,128)(2,1)S(1)}, u32[]{:S(2)}, u32[]{:S(2)}) %collective-permute-start.36) | collective-permute-done | bytes 319520 | tf_op jit(solution)/shard_map/ppermute | solution.py:43
  157.7 3.0 %collective-permute-start.38 = (bf16[208,768]{1,0:T(8,128)(2,1)S(1)}, bf16[208,768]{1,0:T(8,128)(2,1)S(1)}, u32[]{:S(2)}, u32[]{:S(2)}) collective-permute-start(bf16[208,768]{1,0:T(8,128)(2,1)S(1)} %collective-permute-done.36.refs_1_), channel_id=1, source_target_pairs={{0,2},{1,3},{2,0},{3,1},{4,6},{5,7},{6,4},{7,5},{8,10},{9,11},{10,... | collective-permute-start | bytes 958472 | tf_op jit(solution)/shard_map/ppermute | solution.py:43
  (137 shorter events, 60.5 us)
Async XLA Ops:
  0.7 14.8 %collective-permute-start = (bf16[128,768]{1,0:T(8,128)(2,1)}, bf16[128,768]{1,0:T(8,128)(2,1)}, u32[]{:S(2)}, u32[]{:S(2)}) collective-permute-start(bf16[128,768]{1,0:T(8,128)(2,1)} %bitcast.22), channel_id=1, source_target_pairs={{0,8},{8,0},{16,24},{24,16},{1,9},{9,1},{17,25},{25,17},{2,10},{10... | collective-permute-start | bytes 589832 | tf_op jit(solution)/shard_map/ppermute | solution.py:43
  1.3 16.0 %collective-permute-start.1 = (bf16[128,768]{1,0:T(8,128)(2,1)}, bf16[128,768]{1,0:T(8,128)(2,1)}, u32[]{:S(2)}, u32[]{:S(2)}) collective-permute-start(bf16[128,768]{1,0:T(8,128)(2,1)} %bitcast.23), channel_id=1, source_target_pairs={{0,16},{8,24},{16,0},{24,8},{1,17},{9,25},{17,1},{25,9},{2,18},{10... | collective-permute-start | bytes 589832 | tf_op jit(solution)/shard_map/ppermute | solution.py:43
  17.3 14.0 %collective-permute-start.14 = (bf16[192,768]{1,0:T(8,128)(2,1)}, bf16[192,768]{1,0:T(8,128)(2,1)S(1)}, u32[]{:S(2)}, u32[]{:S(2)}) collective-permute-start(bf16[192,768]{1,0:T(8,128)(2,1)} %get-tuple-element.92), channel_id=1, source_target_pairs={{0,24},{8,16},{16,8},{24,0},{1,25},{9,17},{17,9},{25,1},{2,26},{10... | collective-permute-start | bytes 884744 | tf_op jit(solution)/shard_map/ppermute | solution.py:43
  19.0 16.3 %collective-permute-start.9 = (bf16[192,576]{1,0:T(8,128)(2,1)}, bf16[192,576]{1,0:T(8,128)(2,1)S(1)}, u32[]{:S(2)}, u32[]{:S(2)}) collective-permute-start(bf16[192,576]{1,0:T(8,128)(2,1)} %get-tuple-element.82), channel_id=1, source_target_pairs={{0,8},{8,0},{16,24},{24,16},{1,9},{9,1},{17,25},{25,17},{2,10},{10... | collective-permute-start | bytes 663560 | tf_op jit(solution)/shard_map/ppermute | solution.py:43
  19.3 17.9 %collective-permute-start.10 = (bf16[192,576]{1,0:T(8,128)(2,1)}, bf16[192,576]{1,0:T(8,128)(2,1)S(1)}, u32[]{:S(2)}, u32[]{:S(2)}) collective-permute-start(bf16[192,576]{1,0:T(8,128)(2,1)} %get-tuple-element.83), channel_id=1, source_target_pairs={{0,16},{8,24},{16,0},{24,8},{1,17},{9,25},{17,1},{25,9},{2,18},{10... | collective-permute-start | bytes 663560 | tf_op jit(solution)/shard_map/ppermute | solution.py:43
  25.0 16.3 %collective-permute-start.11 = (bf16[192,576]{1,0:T(8,128)(2,1)S(1)}, bf16[192,576]{1,0:T(8,128)(2,1)S(1)}, u32[]{:S(2)}, u32[]{:S(2)}) collective-permute-start(bf16[192,576]{1,0:T(8,128)(2,1)S(1)} %copy-done.10), channel_id=1, source_target_pairs={{0,24},{8,16},{16,8},{24,0},{1,25},{9,17},{17,9},{25,1},{2,26},{10... | collective-permute-start | bytes 663560 | tf_op jit(solution)/shard_map/ppermute | solution.py:43
  53.4 37.9 %collective-permute-start.15 = (bf16[2,272,768]{2,1,0:T(8,128)(2,1)S(1)}, bf16[2,272,768]{2,1,0:T(8,128)(2,1)S(1)}, u32[]{:S(2)}, u32[]{:S(2)}) collective-permute-start(bf16[2,272,768]{2,1,0:T(8,128)(2,1)S(1)} %get-tuple-element.106), channel_id=1, source_target_pairs={{0,8},{8,0},{16,24},{24,16},{1,9},{9,1},{17,25},{25,17},{2,10},{10... | collective-permute-start | bytes 2506760 | tf_op jit(solution)/shard_map/ppermute | solution.py:43
  55.7 14.4 %collective-permute-start.40 = (bf16[2,96,768]{2,1,0:T(8,128)(2,1)S(1)}, bf16[2,96,768]{2,1,0:T(8,128)(2,1)S(1)}, u32[]{:S(2)}, u32[]{:S(2)}) collective-permute-start(bf16[2,96,768]{2,1,0:T(8,128)(2,1)S(1)} %get-tuple-element.135), channel_id=1, source_target_pairs={{0,1},{1,0},{2,3},{3,2},{4,5},{5,4},{6,7},{7,6},{8,9},{9,8},{10,11... | collective-permute-start | bytes 884744 | tf_op jit(solution)/shard_map/ppermute | solution.py:43
  55.9 16.0 %collective-permute-start.29 = (bf16[4,48,768]{2,1,0:T(8,128)(2,1)S(1)}, bf16[4,48,768]{2,1,0:T(8,128)(2,1)S(1)}, u32[]{:S(2)}, u32[]{:S(2)}) collective-permute-start(bf16[4,48,768]{2,1,0:T(8,128)(2,1)S(1)} %get-tuple-element.122), channel_id=1, source_target_pairs={{0,2},{1,3},{2,0},{3,1},{4,6},{5,7},{6,4},{7,5},{8,10},{9,11},{10,... | collective-permute-start | bytes 884744 | tf_op jit(solution)/shard_map/ppermute | solution.py:43
  57.7 18.7 %collective-permute-start.17 = (bf16[4,48,768]{2,1,0:T(8,128)(2,1)S(1)}, bf16[4,48,768]{2,1,0:T(8,128)(2,1)S(1)}, u32[]{:S(2)}, u32[]{:S(2)}) collective-permute-start(bf16[4,48,768]{2,1,0:T(8,128)(2,1)S(1)} %get-tuple-element.108), channel_id=1, source_target_pairs={{0,1},{1,0},{2,3},{3,2},{4,5},{5,4},{6,7},{7,6},{8,9},{9,8},{10,11... | collective-permute-start | bytes 884744 | tf_op jit(solution)/shard_map/ppermute | solution.py:43
  63.8 14.4 %collective-permute-start.19 = (bf16[4,48,768]{2,1,0:T(8,128)(2,1)S(1)}, bf16[4,48,768]{2,1,0:T(8,128)(2,1)S(1)}, u32[]{:S(2)}, u32[]{:S(2)}) collective-permute-start(bf16[4,48,768]{2,1,0:T(8,128)(2,1)S(1)} %shard_map.270), channel_id=1, source_target_pairs={{0,2},{1,3},{2,0},{3,1},{4,6},{5,7},{6,4},{7,5},{8,10},{9,11},{10,... | collective-permute-start | bytes 884744 | tf_op jit(solution)/shard_map/ppermute | solution.py:43
  76.4 16.8 %collective-permute-start.28 = (bf16[4,48,768]{2,1,0:T(8,128)(2,1)S(1)}, bf16[4,48,768]{2,1,0:T(8,128)(2,1)S(1)}, u32[]{:S(2)}, u32[]{:S(2)}) collective-permute-start(bf16[4,48,768]{2,1,0:T(8,128)(2,1)S(1)} %get-tuple-element.120), channel_id=1, source_target_pairs={{0,2},{1,3},{2,0},{3,1},{4,6},{5,7},{6,4},{7,5},{8,10},{9,11},{10,... | collective-permute-start | bytes 884744 | tf_op jit(solution)/shard_map/ppermute | solution.py:43
  78.2 15.0 %collective-permute-start.30 = (bf16[4,48,768]{2,1,0:T(8,128)(2,1)S(1)}, bf16[4,48,768]{2,1,0:T(8,128)(2,1)S(1)}, u32[]{:S(2)}, u32[]{:S(2)}) collective-permute-start(bf16[4,48,768]{2,1,0:T(8,128)(2,1)S(1)} %shard_map.276), channel_id=1, source_target_pairs={{0,1},{1,0},{2,3},{3,2},{4,5},{5,4},{6,7},{7,6},{8,9},{9,8},{10,11... | collective-permute-start | bytes 884744 | tf_op jit(solution)/shard_map/ppermute | solution.py:43
  91.4 28.8 %collective-permute-start.16 = (bf16[272,768]{1,0:T(8,128)(2,1)S(1)}, bf16[272,768]{1,0:T(8,128)(2,1)S(1)}, u32[]{:S(2)}, u32[]{:S(2)}) collective-permute-start(bf16[272,768]{1,0:T(8,128)(2,1)S(1)} %shard_map.269), channel_id=1, source_target_pairs={{0,16},{8,24},{16,0},{24,8},{1,17},{9,25},{17,1},{25,9},{2,18},{10... | collective-permute-start | bytes 1253384 | tf_op jit(solution)/shard_map/ppermute | solution.py:43
  103.7 16.3 %collective-permute-start.24 = (bf16[2,48,768]{2,1,0:T(8,128)(2,1)S(1)}, bf16[2,48,768]{2,1,0:T(8,128)(2,1)S(1)}, u32[]{:S(2)}, u32[]{:S(2)}) collective-permute-start(bf16[2,48,768]{2,1,0:T(8,128)(2,1)S(1)} %shard_map.273.refs_0_), channel_id=1, source_target_pairs={{0,4},{1,5},{2,6},{3,7},{4,0},{5,1},{6,2},{7,3},{8,12},{9,13},{10,... | collective-permute-start | bytes 442376 | tf_op jit(solution)/shard_map/ppermute | solution.py:43
  112.8 18.7 %collective-permute-start.44 = (bf16[2,96,768]{2,1,0:T(8,128)(2,1)S(1)}, bf16[2,96,768]{2,1,0:T(8,128)(2,1)S(1)}, u32[]{:S(2)}, u32[]{:S(2)}) collective-permute-start(bf16[2,96,768]{2,1,0:T(8,128)(2,1)S(1)} %shard_map.285.refs_0_), channel_id=1, source_target_pairs={{0,2},{1,3},{2,0},{3,1},{4,6},{5,7},{6,4},{7,5},{8,10},{9,11},{10,... | collective-permute-start | bytes 884744 | tf_op jit(solution)/shard_map/ppermute | solution.py:43
  120.0 17.1 %collective-permute-start.25 = (bf16[4,48,768]{2,1,0:T(8,128)(2,1)S(1)}, bf16[4,48,768]{2,1,0:T(8,128)(2,1)S(1)}, u32[]{:S(2)}, u32[]{:S(2)}) collective-permute-start(bf16[4,48,768]{2,1,0:T(8,128)(2,1)S(1)} %bitcast.26), channel_id=1, source_target_pairs={{0,2},{1,3},{2,0},{3,1},{4,6},{5,7},{6,4},{7,5},{8,10},{9,11},{10,... | collective-permute-start | bytes 884744 | tf_op jit(solution)/shard_map/ppermute | solution.py:43
  120.5 18.1 %collective-permute-start.35 = (bf16[112,768]{1,0:T(8,128)(2,1)S(1)}, bf16[112,768]{1,0:T(8,128)(2,1)S(1)}, u32[]{:S(2)}, u32[]{:S(2)}) collective-permute-start(bf16[112,768]{1,0:T(8,128)(2,1)S(1)} %shard_map.279.refs_0_), channel_id=1, source_target_pairs={{0,4},{1,5},{2,6},{3,7},{4,0},{5,1},{6,2},{7,3},{8,12},{9,13},{10,... | collective-permute-start | bytes 516104 | tf_op jit(solution)/shard_map/ppermute | solution.py:43
  124.0 15.5 %collective-permute-start.45 = (bf16[2,96,768]{2,1,0:T(8,128)(2,1)S(1)}, bf16[2,96,768]{2,1,0:T(8,128)(2,1)S(1)}, u32[]{:S(2)}, u32[]{:S(2)}) collective-permute-start(bf16[2,96,768]{2,1,0:T(8,128)(2,1)S(1)} %shard_map.285.refs_0_), channel_id=1, source_target_pairs={{0,1},{1,0},{2,3},{3,2},{4,5},{5,4},{6,7},{7,6},{8,9},{9,8},{10,11... | collective-permute-start | bytes 884744 | tf_op jit(solution)/shard_map/ppermute | solution.py:43
  125.5 37.7 %collective-permute-start.26 = (bf16[4,48,768]{2,1,0:T(8,128)(2,1)S(1)}, bf16[4,48,768]{2,1,0:T(8,128)(2,1)S(1)}, u32[]{:S(2)}, u32[]{:S(2)}) collective-permute-start(bf16[4,48,768]{2,1,0:T(8,128)(2,1)S(1)} %bitcast.27), channel_id=1, source_target_pairs={{0,1},{1,0},{2,3},{3,2},{4,5},{5,4},{6,7},{7,6},{8,9},{9,8},{10,11... | collective-permute-start | bytes 884744 | tf_op jit(solution)/shard_map/ppermute | solution.py:43
  131.5 30.1 %collective-permute-start.46 = (bf16[2,96,768]{2,1,0:T(8,128)(2,1)S(1)}, bf16[2,96,768]{2,1,0:T(8,128)(2,1)S(1)}, u32[]{:S(2)}, u32[]{:S(2)}) collective-permute-start(bf16[2,96,768]{2,1,0:T(8,128)(2,1)S(1)} %collective-permute-done.44.refs_1_), channel_id=1, source_target_pairs={{0,1},{1,0},{2,3},{3,2},{4,5},{5,4},{6,7},{7,6},{8,9},{9,8},{10,11... | collective-permute-start | bytes 884744 | tf_op jit(solution)/shard_map/ppermute | solution.py:43
  137.1 26.2 %collective-permute-start.27 = (bf16[4,48,768]{2,1,0:T(8,128)(2,1)S(1)}, bf16[4,48,768]{2,1,0:T(8,128)(2,1)S(1)}, u32[]{:S(2)}, u32[]{:S(2)}) collective-permute-start(bf16[4,48,768]{2,1,0:T(8,128)(2,1)S(1)} %collective-permute-done.25.refs_1_), channel_id=1, source_target_pairs={{0,1},{1,0},{2,3},{3,2},{4,5},{5,4},{6,7},{7,6},{8,9},{9,8},{10,11... | collective-permute-start | bytes 884744 | tf_op jit(solution)/shard_map/ppermute | solution.py:43
  138.7 19.0 %collective-permute-start.36 = (bf16[208,768]{1,0:T(8,128)(2,1)S(1)}, bf16[208,768]{1,0:T(8,128)(2,1)S(1)}, u32[]{:S(2)}, u32[]{:S(2)}) collective-permute-start(bf16[208,768]{1,0:T(8,128)(2,1)S(1)} %shard_map.280.refs_0_), channel_id=1, source_target_pairs={{0,1},{1,0},{2,3},{3,2},{4,5},{5,4},{6,7},{7,6},{8,9},{9,8},{10,11... | collective-permute-start | bytes 958472 | tf_op jit(solution)/shard_map/ppermute | solution.py:43
  139.5 25.6 %collective-permute-start.37 = (bf16[208,768]{1,0:T(8,128)(2,1)S(1)}, bf16[208,768]{1,0:T(8,128)(2,1)S(1)}, u32[]{:S(2)}, u32[]{:S(2)}) collective-permute-start(bf16[208,768]{1,0:T(8,128)(2,1)S(1)} %shard_map.280.refs_0_), channel_id=1, source_target_pairs={{0,2},{1,3},{2,0},{3,1},{4,6},{5,7},{6,4},{7,5},{8,10},{9,11},{10,... | collective-permute-start | bytes 958472 | tf_op jit(solution)/shard_map/ppermute | solution.py:43
  (34 other events, 315.4 us)

commit v2 on v1

--- a/solution.py
+++ b/solution.py
@@ -83,9 +83,11 @@
                 :, width + a : width + a + HEAD_DIM
             ]
         scr[t, :, 2 * rows : 3 * rows] = wq[:, 2 * width + base : 2 * width + base + rows]
+    half = q2.shape[0]
+    mine = pl.ds(pl.multiple_of(bit_of("rep", 1) * half, 16), half)
     for k, (q, u) in enumerate(((q0, u0), (q1, u1), (q2, u2), (q3, u3))):
         t = me ^ k
-        q[...] = scr[t]
+        q[...] = scr[t] if k < 2 else scr[t, mine, :]
         u[...] = wu[:, pl.ds(pl.multiple_of(t * wide, 128), wide)]
 
 
@@ -141,7 +143,7 @@
     csum[...] = jnp.sum(as_float(cot[...]), axis=0, keepdims=True)
 
 
-def att_kernel(order, hid, hid_t, cot, datt, q0, q1, q2, q3, bq, ca, sa, sb, segc, segr,
+def att_kernel(order, hid, hid_t, cot, datt, q0, q1, q2, q2r, q3, q3r, bq, ca, sa, sb, segc, segr,
                sa_o, sb_o, ka_o, kb_o, att_o, dproj_o, wfull, bsum, neg, grid):
     me = lax.axis_index("shard")
     first, second = (bit_of("rep", bit) for bit in order)
@@ -149,8 +151,10 @@
     length, width = cot.shape
     two = 2 * HEAD_DIM
     n_h = rows // HEAD_DIM
-    for j, q in enumerate((q0, q1, q2, q3)):
-        wfull[pl.ds(pl.multiple_of((me ^ j) * rows, 16), rows), :] = q[...]
+    side = bit_of("rep", 1)
+    for j, part, q in ((0, 0, q0), (1, 0, q1), (2, side, q2), (2, 1 - side, q2r), (3, side, q3), (3, 1 - side, q3r)):
+        n = q.shape[0]
+        wfull[pl.ds(pl.multiple_of((me ^ j) * rows + part * n, 16), n), :] = q[...]
     col = lax.broadcasted_iota(jnp.int32, (length, length), 1)
     row = lax.broadcasted_iota(jnp.int32, (length, length), 0)
     neg[...] = jnp.where((col <= row) & (segc[...] == segr[...]), 0.0, -jnp.inf)
@@ -226,15 +230,16 @@
 
 
 def mlp3_kernel(x0, x1, x2, x3, att, activ, dproj, dpre, wo, wd, wq, wu, vec,
-                bsum, csum, bup, send, keep, vecs):
+                bsum, csum, bup, send, keep, vecs, out_s, one_s, two_s):
     me = lax.axis_index("shard")
     count = x0.shape[0]
     total = [None] * 4
+    out_s[...] = dot(att[...], wo[...], ((1,), (0,))) + dot(activ[...], wd[...], ((1,), (0,)))
+    one_s[...] = dot(dproj[...], wq[...], ((1,), (1,)))
+    two_s[...] = dot(dpre[...], wu[...], ((1,), (1,)))
     for j, x in enumerate((x0, x1, x2, x3)):
         part = pl.ds(pl.multiple_of((me ^ j) * count, count), count)
-        out = dot(att[part, :], wo[...], ((1,), (0,))) + dot(activ[part, :], wd[...], ((1,), (0,)))
-        one = dot(dproj[part, :], wq[...], ((1,), (1,)))
-        two = dot(dpre[part, :], wu[...], ((1,), (1,)))
+        out, one, two = out_s[part, :], one_s[part, :], two_s[part, :]
         normed = normed_of(x)
         target = keep if j % 2 == 0 else send
         target[j // 2, :count, :] = out.astype(BF)
@@ -341,11 +346,18 @@
             out[pl.ds(start, n_r), :] = as_float(value[t])
 
 
-def final_up_kernel(order, p0, p1, p2, p3, out, vec):
+def final_up_kernel(order, p0, p1, p2, p3, out, g1, b1, g2, b2, tot_q, cot_a, cot_b, tot_u, vec):
     n_r = out.shape[0] // 4
     wide = out.shape[1] // 4
     v0, v1, v2, v3 = (as_float(p[4 * n_r :, :]) for p in (p0, p1, p2, p3))
     vec[...] = (v0 + v1) + (v2 + v3)
+    rows = g1.shape[0]
+    for k, ref in enumerate((g1, b1, g2, b2)):
+        ref[...] = vec[0, rows * k : rows * (k + 1)]
+    tot_q[...] = vec[1, : 3 * rows]
+    cot_a[...] = vec[1, 3 * rows :]
+    cot_b[...] = vec[1, 3 * rows :]
+    tot_u[...] = vec[2, :]
     for value, half, b in quarters(order, (p0, p1, p2, p3)):
         start = pl.multiple_of((half * 2 + b) * n_r, 8)
         for s in range(4):
@@ -407,18 +419,22 @@
         x = gather(tokens_in)
         packed = call(
             pack_kernel,
-            [((rows, 3 * rows), BF)] * 4 + [((rows, wide), BF)] * 4 + [((8, 3 * rows), F32)],
+            [((rows, 3 * rows), BF)] * 2
+            + [((rows // 2, 3 * rows), BF)] * 2
+            + [((rows, wide), BF)] * 4
+            + [((8, 3 * rows), F32)],
             (w_qkv, w_up, positions, ln1_gain, ln1_bias, ln2_gain, ln2_bias, b_out, b_down, b_qkv),
             scratch=[((4, rows, 3 * rows), BF)],
             limit=62,
         )
-        q_w = (packed[0], *(to(j, packed[j]) for j in (1, 2, 3)))
+        q_two, q_three = to(2, packed[2]), to(3, packed[3])
+        q_w = (packed[0], to(1, packed[1]), q_two, swap(q_two, "rep", reps, 1), q_three, swap(q_three, "rep", reps, 1))
         c = gather(cotan_own)
         u_w = (packed[4], *(to(j, packed[4 + j]) for j in (1, 2, 3)))
 
         small = gather(packed[8])
         first, second, third = bits[:3]
-        order_att, order_down, order_up = (first, second), (first, second), (second, first)
+        order_att, order_down, order_up = (first, second), (second, first), (first, second)
         sub = rows // 4
         n_c = width // rows
 
@@ -477,7 +493,7 @@
             [((2, 2 * count + 16, width), BF)] * 2,
             (*x, att, activ, dproj, dpre, w_out, w_down, wq_full, wu_full, vec_in,
              bsum, csum, bup_sum),
-            scratch=[((4, 16, width), F32)],
+            scratch=[((4, 16, width), F32)] + [((length, width), F32)] * 3,
             flops=3_000_000_000,
             limit=24,
         )
@@ -549,14 +565,14 @@
             lambda *refs: final_qkv_kernel(order_att, *refs), [((rows, 3 * width), F32), ((rows, width), F32)], own_c
         )
         (tot_down,) = call(lambda *refs: final_down_kernel(order_down, *refs), [((wide, width), F32)], own_a)
-        tot_up, vec = call(
-            lambda *refs: final_up_kernel(order_up, *refs), [((rows, shards * wide), F32), (vec_own.shape, F32)], own_b
-        )
-
-        g1, bb1, g2, bb2 = [vec[0, k * rows : (k + 1) * rows] for k in range(4)]
-        tot_bqkv = vec[1, : 3 * rows]
-        tot_cot = vec[1, 3 * rows :]
-        tot_bup = vec[2]
+        tot_up, g1, bb1, g2, bb2, tot_bqkv, tot_cot, tot_cot_two, tot_bup = call(
+            lambda *refs: final_up_kernel(order_up, *refs),
+            [((rows, shards * wide), F32)]
+            + [((n,), F32) for n in (rows, rows, rows, rows, 3 * rows, rows, rows, wide)],
+            own_b,
+            scratch=[(vec_own.shape, F32)],
+        )
+
         return (
             output[None],
             d_input[None],
@@ -567,7 +583,7 @@
             tot_up,
             tot_bup,
             tot_down,
-            tot_cot,
+            tot_cot_two,
             g1,
             bb1,
             g2,

time: 171 us -> 159 us (0.930)
  waiting for transfers between devices: 72.9 us -> 66.9 us
  starting transfers between devices: 62.2 us -> 57.9 us
  local copies, waits for them, and re-layouts: 3.35 us -> 0.98 us
    ppermute x47 -> x49, waiting for transfers between devices: 72.9 us -> 66.9 us  [swap(): return lax.ppermute(value, axis, [(i, i ^ bit) for i in range(size)])]
    ppermute x47 -> x49, starting transfers between devices: 62.2 us -> 57.9 us  [swap(): return lax.ppermute(value, axis, [(i, i ^ bit) for i in range(size)])]
    slice x3 -> x0, local copies, waits for them, and re-layouts: 1.85 us -> none  [the longest x1 0.64 us: body(): g1, bb1, g2, bb2 = [vec[0, k * rows:(k + 1) * rows] for k in range(4)]]
  transfers between devices with their start and end apart: 47 -> 49, of which waited for: 21 -> 19; matrix products, arithmetic and copies ran while one was open for 2% -> 2% of each run, Pallas kernels for 8% -> 9%
where the time goes in v2:
time: 159 us; the launch traced here: 157 us
  waiting for transfers between devices  66.9 us (42%)
  starting transfers between devices  57.9 us (36%)
  Pallas kernels  27.5 us (17%)
  other arithmetic  2.73 us (2%)
    ppermute x49, waiting for transfers between devices, swap(): return lax.ppermute(value, axis, [(i, i ^ bit) for i in range(size)])  66.9 us
    ppermute x49, starting transfers between devices, swap(): return lax.ppermute(value, axis, [(i, i ^ bit) for i in range(size)])  57.9 us
    pallas_call x24, Pallas kernels, call(): pl.pallas_call(kernel, out_shape=shapes, scratch_shapes=[pltpu.VMEM(s, d)...  27.5 us
  transfers between devices with their start and end apart: 49, of which 19 were waited for; matrix products, arithmetic and copies ran while one was open for 2% of the time, Pallas kernels for 9%

profile of v2, /device:TPU:0, one launch (start us, length us, event | category | flops | bytes accessed | tf_op | source)
XLA Modules:
  0.0 157.1 jit_solution(16985905119485942395)
XLA Ops:
  0.7 3.0 %collective-permute-start.1 = (bf16[128,768]{1,0:T(8,128)(2,1)}, bf16[128,768]{1,0:T(8,128)(2,1)}, u32[]{:S(2)}, u32[]{:S(2)}) collective-permute-start(bf16[128,768]{1,0:T(8,128)(2,1)} %bitcast.17), channel_id=1, source_target_pairs={{0,16},{8,24},{16,0},{24,8},{1,17},{9,25},{17,1},{25,9},{2,18},{10... | collective-permute-start | bytes 589832 | tf_op jit(solution)/shard_map/ppermute | solution.py:43
  4.3 3.3 %shard_map.263 = (bf16[192,576]{1,0:T(8,128)(2,1)}, bf16[192,576]{1,0:T(8,128)(2,1)}, bf16[96,576]{1,0:T(8,128)(2,1)}, bf16[96,576]{1,0:T(8,128)(2,1)}, bf16[192...) custom-call(bf16[192,2304]{1,0:T(8,128)(2,1)} %wq.1, ...), custom_call_target="tpu_custom_call" | custom-call | bytes 3929984 | tf_op jit(solution)/shard_map/pallas_call | solution.py:53
  10.9 2.4 %collective-permute-done.4.c2 = bf16[128,768]{1,0:T(8,128)(2,1)} collective-permute-done((bf16[128,768]{1,0:T(8,128)(2,1)}, bf16[128,768]{1,0:T(8,128)(2,1)}, u32[]{:S(2)}, u32[]{:S(2)}) %collective-permute-start.4) | collective-permute-done | bytes 196640 | tf_op jit(solution)/shard_map/ppermute | solution.py:43
  19.8 3.1 %shard_map.264 = (bf16[512,768]{1,0:T(8,128)(2,1)S(1)}, bf16[768,512]{1,0:T(8,128)(2,1)S(1)}, bf16[512,768]{1,0:T(8,128)(2,1)S(1)}, bf16[768,512]{1,0:T(8,128)(2...) custom-call(bf16[128,768]{1,0:T(8,128)(2,1)S(1)} %bitcast.19, ...), custom_call_target="tpu_custom_call" | custom-call | flops 1000000000 | bytes 8854784 | tf_op jit(solution)/shard_map/pallas_call | solution.py:53
  26.4 3.8 %collective-permute-done.15.refs_4_ = bf16[192,768]{1,0:T(8,128)(2,1)S(1)} collective-permute-done((bf16[192,768]{1,0:T(8,128)(2,1)}, bf16[192,768]{1,0:T(8,128)(2,1)S(1)}, u32[]{:S(2)}, u32[]{:S(2)}) %collective-permute-start.15) | collective-permute-done | bytes 294944 | tf_op jit(solution)/shard_map/ppermute | solution.py:43
  30.2 5.1 %collective-permute-done.16.refs_5_ = bf16[192,768]{1,0:T(8,128)(2,1)S(1)} collective-permute-done((bf16[192,768]{1,0:T(8,128)(2,1)}, bf16[192,768]{1,0:T(8,128)(2,1)S(1)}, u32[]{:S(2)}, u32[]{:S(2)}) %collective-permute-start.16) | collective-permute-done | bytes 294944 | tf_op jit(solution)/shard_map/ppermute | solution.py:43
  38.3 7.0 %shard_map.265 = (bf16[4,48,768]{2,1,0:T(8,128)(2,1)S(1)}, bf16[4,48,768]{2,1,0:T(8,128)(2,1)S(1)}, bf16[4,48,768]{2,1,0:T(8,128)(2,1)S(1)}, bf16[4,48,768]{2,1,...) custom-call(bf16[512,768]{1,0:T(8,128)(2,1)S(1)} %get-tuple-element., ...), custom_call_target="tpu_custom_call" | custom-call | flops 4000000000 | bytes 7086592 | tf_op jit(solution)/shard_map/pallas_call | solution.py:53
  45.3 5.0 %shard_map.268 = (bf16[2,272,768]{2,1,0:T(8,128)(2,1)S(1)}, bf16[2,272,768]{2,1,0:T(8,128)(2,1)S(1)}) custom-call(bf16[128,768]{1,0:T(8,128)(2,1)S(1)} %bitcast.20, bf16[128,768]{1,0:T(8,128)(2,1)} %collective-permute-done.x1, bf16[128,768]{1,0:T(8,128)(2,1)} %collective-permute-done.1.x2, bf16[128,768]{1,0:T(8,128)(2,1)S(1)} %copy-done.8, ...), custom_call_target="tpu_custom_call" | custom-call | flops 3000000000 | bytes 8388864 | tf_op jit(solution)/shard_map/pallas_call | solution.py:53
  56.1 4.5 %collective-permute-done.20.got = bf16[4,48,768]{2,1,0:T(8,128)(2,1)S(1)} collective-permute-done((bf16[4,48,768]{2,1,0:T(8,128)(2,1)S(1)}, bf16[4,48,768]{2,1,0:T(8,128)(2,1)S(1)}, u32[]{:S(2)}, u32[]{:S(2)}) %collective-permute-start.20) | collective-permute-done | bytes 294944 | tf_op jit(solution)/shard_map/ppermute | solution.py:43
  62.9 4.1 %collective-permute-done.31.got = bf16[4,48,768]{2,1,0:T(8,128)(2,1)S(1)} collective-permute-done((bf16[4,48,768]{2,1,0:T(8,128)(2,1)S(1)}, bf16[4,48,768]{2,1,0:T(8,128)(2,1)S(1)}, u32[]{:S(2)}, u32[]{:S(2)}) %collective-permute-start.31) | collective-permute-done | bytes 294944 | tf_op jit(solution)/shard_map/ppermute | solution.py:43
  68.8 4.5 %collective-permute-done.19.got = bf16[4,48,768]{2,1,0:T(8,128)(2,1)S(1)} collective-permute-done((bf16[4,48,768]{2,1,0:T(8,128)(2,1)S(1)}, bf16[4,48,768]{2,1,0:T(8,128)(2,1)S(1)}, u32[]{:S(2)}, u32[]{:S(2)}) %collective-permute-start.19) | collective-permute-done | bytes 294944 | tf_op jit(solution)/shard_map/ppermute | solution.py:43
  76.9 2.7 %collective-permute-done.43.refs_2_ = bf16[2,96,768]{2,1,0:T(8,128)(2,1)S(1)} collective-permute-done((bf16[2,96,768]{2,1,0:T(8,128)(2,1)S(1)}, bf16[2,96,768]{2,1,0:T(8,128)(2,1)S(1)}, u32[]{:S(2)}, u32[]{:S(2)}) %collective-permute-start.43) | collective-permute-done | bytes 294944 | tf_op jit(solution)/shard_map/ppermute | solution.py:43
  83.8 2.8 %collective-permute-start.44 = (bf16[96,768]{1,0:T(8,128)(2,1)S(1)}, bf16[96,768]{1,0:T(8,128)(2,1)S(1)}, u32[]{:S(2)}, u32[]{:S(2)}) collective-permute-start(bf16[96,768]{1,0:T(8,128)(2,1)S(1)} %get-tuple-element.146), channel_id=1, source_target_pairs={{0,4},{1,5},{2,6},{3,7},{4,0},{5,1},{6,2},{7,3},{8,12},{9,13},{10,... | collective-permute-start | bytes 442376 | tf_op jit(solution)/shard_map/ppermute | solution.py:43
  89.8 6.5 %collective-permute-done.44.got = bf16[96,768]{1,0:T(8,128)(2,1)S(1)} collective-permute-done((bf16[96,768]{1,0:T(8,128)(2,1)S(1)}, bf16[96,768]{1,0:T(8,128)(2,1)S(1)}, u32[]{:S(2)}, u32[]{:S(2)}) %collective-permute-start.44) | collective-permute-done | bytes 147488 | tf_op jit(solution)/shard_map/ppermute | solution.py:43
  96.4 4.6 %collective-permute-done.25.got = bf16[2,48,768]{2,1,0:T(8,128)(2,1)S(1)} collective-permute-done((bf16[2,48,768]{2,1,0:T(8,128)(2,1)S(1)}, bf16[2,48,768]{2,1,0:T(8,128)(2,1)S(1)}, u32[]{:S(2)}, u32[]{:S(2)}) %collective-permute-start.25) | collective-permute-done | bytes 147488 | tf_op jit(solution)/shard_map/ppermute | solution.py:43
  103.2 2.4 %collective-permute-done.34.refs_2_ = bf16[48,768]{1,0:T(8,128)(2,1)S(1)} collective-permute-done((bf16[48,768]{1,0:T(8,128)(2,1)S(1)}, bf16[48,768]{1,0:T(8,128)(2,1)S(1)}, u32[]{:S(2)}, u32[]{:S(2)}) %collective-permute-start.34) | collective-permute-done | bytes 73760 | tf_op jit(solution)/shard_map/ppermute | solution.py:43
  107.2 2.9 %collective-permute-start.36 = (bf16[2,48,768]{2,1,0:T(8,128)(2,1)S(1)}, bf16[2,48,768]{2,1,0:T(8,128)(2,1)S(1)}, u32[]{:S(2)}, u32[]{:S(2)}) collective-permute-start(bf16[2,48,768]{2,1,0:T(8,128)(2,1)S(1)} %get-tuple-element.135), channel_id=1, source_target_pairs={{0,4},{1,5},{2,6},{3,7},{4,0},{5,1},{6,2},{7,3},{8,12},{9,13},{10,... | collective-permute-start | bytes 442376 | tf_op jit(solution)/shard_map/ppermute | solution.py:43
  111.9 6.1 %collective-permute-start.27 = (bf16[4,48,768]{2,1,0:T(8,128)(2,1)S(1)}, bf16[4,48,768]{2,1,0:T(8,128)(2,1)S(1)}, u32[]{:S(2)}, u32[]{:S(2)}) collective-permute-start(bf16[4,48,768]{2,1,0:T(8,128)(2,1)S(1)} %bitcast.21), channel_id=1, source_target_pairs={{0,2},{1,3},{2,0},{3,1},{4,6},{5,7},{6,4},{7,5},{8,10},{9,11},{10,... | collective-permute-start | bytes 884744 | tf_op jit(solution)/shard_map/ppermute | solution.py:43
  118.3 2.9 %collective-permute-start.37 = (bf16[112,768]{1,0:T(8,128)(2,1)S(1)}, bf16[112,768]{1,0:T(8,128)(2,1)S(1)}, u32[]{:S(2)}, u32[]{:S(2)}) collective-permute-start(bf16[112,768]{1,0:T(8,128)(2,1)S(1)} %shard_map.279.refs_0_), channel_id=1, source_target_pairs={{0,4},{1,5},{2,6},{3,7},{4,0},{5,1},{6,2},{7,3},{8,12},{9,13},{10,... | collective-permute-start | bytes 516104 | tf_op jit(solution)/shard_map/ppermute | solution.py:43
  121.2 2.9 %collective-permute-start.47 = (bf16[2,96,768]{2,1,0:T(8,128)(2,1)S(1)}, bf16[2,96,768]{2,1,0:T(8,128)(2,1)S(1)}, u32[]{:S(2)}, u32[]{:S(2)}) collective-permute-start(bf16[2,96,768]{2,1,0:T(8,128)(2,1)S(1)} %shard_map.285.refs_0_), channel_id=1, source_target_pairs={{0,2},{1,3},{2,0},{3,1},{4,6},{5,7},{6,4},{7,5},{8,10},{9,11},{10,... | collective-permute-start | bytes 884744 | tf_op jit(solution)/shard_map/ppermute | solution.py:43
  125.7 3.9 %collective-permute-done.27.refs_1_ = bf16[4,48,768]{2,1,0:T(8,128)(2,1)S(1)} collective-permute-done((bf16[4,48,768]{2,1,0:T(8,128)(2,1)S(1)}, bf16[4,48,768]{2,1,0:T(8,128)(2,1)S(1)}, u32[]{:S(2)}, u32[]{:S(2)}) %collective-permute-start.27) | collective-permute-done | bytes 294944 | tf_op jit(solution)/shard_map/ppermute | solution.py:43
  130.1 3.8 %collective-permute-start.38 = (bf16[208,768]{1,0:T(8,128)(2,1)S(1)}, bf16[208,768]{1,0:T(8,128)(2,1)S(1)}, u32[]{:S(2)}, u32[]{:S(2)}) collective-permute-start(bf16[208,768]{1,0:T(8,128)(2,1)S(1)} %shard_map.280.refs_0_), channel_id=1, source_target_pairs={{0,2},{1,3},{2,0},{3,1},{4,6},{5,7},{6,4},{7,5},{8,10},{9,11},{10,... | collective-permute-start | bytes 958472 | tf_op jit(solution)/shard_map/ppermute | solution.py:43
  136.4 11.1 %collective-permute-done.38.refs_1_ = bf16[208,768]{1,0:T(8,128)(2,1)S(1)} collective-permute-done((bf16[208,768]{1,0:T(8,128)(2,1)S(1)}, bf16[208,768]{1,0:T(8,128)(2,1)S(1)}, u32[]{:S(2)}, u32[]{:S(2)}) %collective-permute-start.38) | collective-permute-done | bytes 319520 | tf_op jit(solution)/shard_map/ppermute | solution.py:43
  152.3 3.1 %collective-permute-done.40.refs_3_ = bf16[208,768]{1,0:T(8,128)(2,1)S(1)} collective-permute-done((bf16[208,768]{1,0:T(8,128)(2,1)S(1)}, bf16[208,768]{1,0:T(8,128)(2,1)S(1)}, u32[]{:S(2)}, u32[]{:S(2)}) %collective-permute-start.40) | collective-permute-done | bytes 319520 | tf_op jit(solution)/shard_map/ppermute | solution.py:43
  (139 shorter events, 54.4 us)
Async XLA Ops:
  3.8 13.0 %collective-permute-start = (bf16[128,768]{1,0:T(8,128)(2,1)}, bf16[128,768]{1,0:T(8,128)(2,1)}, u32[]{:S(2)}, u32[]{:S(2)}) collective-permute-start(bf16[128,768]{1,0:T(8,128)(2,1)} %bitcast.18), channel_id=1, source_target_pairs={{0,8},{8,0},{16,24},{24,16},{1,9},{9,1},{17,25},{25,17},{2,10},{10... | collective-permute-start | bytes 589832 | tf_op jit(solution)/shard_map/ppermute | solution.py:43
  3.8 13.0 %collective-permute-start.3 = (bf16[128,768]{1,0:T(8,128)(2,1)}, bf16[128,768]{1,0:T(8,128)(2,1)}, u32[]{:S(2)}, u32[]{:S(2)}) collective-permute-start(bf16[128,768]{1,0:T(8,128)(2,1)} %bitcast.25), channel_id=1, source_target_pairs={{0,8},{8,0},{16,24},{24,16},{1,9},{9,1},{17,25},{25,17},{2,10},{10... | collective-permute-start | bytes 589832 | tf_op jit(solution)/shard_map/ppermute | solution.py:43
  17.2 13.0 %collective-permute-start.15 = (bf16[192,768]{1,0:T(8,128)(2,1)}, bf16[192,768]{1,0:T(8,128)(2,1)S(1)}, u32[]{:S(2)}, u32[]{:S(2)}) collective-permute-start(bf16[192,768]{1,0:T(8,128)(2,1)} %get-tuple-element.98), channel_id=1, source_target_pairs={{0,16},{8,24},{16,0},{24,8},{1,17},{9,25},{17,1},{25,9},{2,18},{10... | collective-permute-start | bytes 884744 | tf_op jit(solution)/shard_map/ppermute | solution.py:43
  19.0 16.3 %collective-permute-start.16 = (bf16[192,768]{1,0:T(8,128)(2,1)}, bf16[192,768]{1,0:T(8,128)(2,1)S(1)}, u32[]{:S(2)}, u32[]{:S(2)}) collective-permute-start(bf16[192,768]{1,0:T(8,128)(2,1)} %get-tuple-element.99), channel_id=1, source_target_pairs={{0,24},{8,16},{16,8},{24,0},{1,25},{9,17},{17,9},{25,1},{2,26},{10... | collective-permute-start | bytes 884744 | tf_op jit(solution)/shard_map/ppermute | solution.py:43
  24.0 14.3 %collective-permute-start.9 = (bf16[192,576]{1,0:T(8,128)(2,1)S(1)}, bf16[192,576]{1,0:T(8,128)(2,1)S(1)}, u32[]{:S(2)}, u32[]{:S(2)}) collective-permute-start(bf16[192,576]{1,0:T(8,128)(2,1)S(1)} %copy-done.11), channel_id=1, source_target_pairs={{0,8},{8,0},{16,24},{24,16},{1,9},{9,1},{17,25},{25,17},{2,10},{10... | collective-permute-start | bytes 663560 | tf_op jit(solution)/shard_map/ppermute | solution.py:43
  24.4 13.9 %collective-permute-start.11 = (bf16[96,576]{1,0:T(8,128)(2,1)S(1)}, bf16[96,576]{1,0:T(8,128)(2,1)S(1)}, u32[]{:S(2)}, u32[]{:S(2)}) collective-permute-start(bf16[96,576]{1,0:T(8,128)(2,1)S(1)} %collective-permute-done.10.refs_6_), channel_id=1, source_target_pairs={{0,1},{1,0},{2,3},{3,2},{4,5},{5,4},{6,7},{7,6},{8,9},{9,8},{10,11... | collective-permute-start | bytes 331784 | tf_op jit(solution)/shard_map/ppermute | solution.py:43
  50.3 38.0 %collective-permute-start.17 = (bf16[2,272,768]{2,1,0:T(8,128)(2,1)S(1)}, bf16[2,272,768]{2,1,0:T(8,128)(2,1)S(1)}, u32[]{:S(2)}, u32[]{:S(2)}) collective-permute-start(bf16[2,272,768]{2,1,0:T(8,128)(2,1)S(1)} %get-tuple-element.113), channel_id=1, source_target_pairs={{0,8},{8,0},{16,24},{24,16},{1,9},{9,1},{17,25},{25,17},{2,10},{10... | collective-permute-start | bytes 2506760 | tf_op jit(solution)/shard_map/ppermute | solution.py:43
  54.6 18.7 %collective-permute-start.19 = (bf16[4,48,768]{2,1,0:T(8,128)(2,1)S(1)}, bf16[4,48,768]{2,1,0:T(8,128)(2,1)S(1)}, u32[]{:S(2)}, u32[]{:S(2)}) collective-permute-start(bf16[4,48,768]{2,1,0:T(8,128)(2,1)S(1)} %get-tuple-element.115), channel_id=1, source_target_pairs={{0,1},{1,0},{2,3},{3,2},{4,5},{5,4},{6,7},{7,6},{8,9},{9,8},{10,11... | collective-permute-start | bytes 884744 | tf_op jit(solution)/shard_map/ppermute | solution.py:43
  60.7 14.3 %collective-permute-start.21 = (bf16[4,48,768]{2,1,0:T(8,128)(2,1)S(1)}, bf16[4,48,768]{2,1,0:T(8,128)(2,1)S(1)}, u32[]{:S(2)}, u32[]{:S(2)}) collective-permute-start(bf16[4,48,768]{2,1,0:T(8,128)(2,1)S(1)} %shard_map.270), channel_id=1, source_target_pairs={{0,2},{1,3},{2,0},{3,1},{4,6},{5,7},{6,4},{7,5},{8,10},{9,11},{10,... | collective-permute-start | bytes 884744 | tf_op jit(solution)/shard_map/ppermute | solution.py:43
  62.6 14.2 %collective-permute-start.41 = (bf16[2,96,768]{2,1,0:T(8,128)(2,1)S(1)}, bf16[2,96,768]{2,1,0:T(8,128)(2,1)S(1)}, u32[]{:S(2)}, u32[]{:S(2)}) collective-permute-start(bf16[2,96,768]{2,1,0:T(8,128)(2,1)S(1)} %get-tuple-element.142), channel_id=1, source_target_pairs={{0,2},{1,3},{2,0},{3,1},{4,6},{5,7},{6,4},{7,5},{8,10},{9,11},{10,... | collective-permute-start | bytes 884744 | tf_op jit(solution)/shard_map/ppermute | solution.py:43
  73.3 16.2 %collective-permute-start.30 = (bf16[4,48,768]{2,1,0:T(8,128)(2,1)S(1)}, bf16[4,48,768]{2,1,0:T(8,128)(2,1)S(1)}, u32[]{:S(2)}, u32[]{:S(2)}) collective-permute-start(bf16[4,48,768]{2,1,0:T(8,128)(2,1)S(1)} %get-tuple-element.127), channel_id=1, source_target_pairs={{0,1},{1,0},{2,3},{3,2},{4,5},{5,4},{6,7},{7,6},{8,9},{9,8},{10,11... | collective-permute-start | bytes 884744 | tf_op jit(solution)/shard_map/ppermute | solution.py:43
  75.1 14.4 %collective-permute-start.32 = (bf16[4,48,768]{2,1,0:T(8,128)(2,1)S(1)}, bf16[4,48,768]{2,1,0:T(8,128)(2,1)S(1)}, u32[]{:S(2)}, u32[]{:S(2)}) collective-permute-start(bf16[4,48,768]{2,1,0:T(8,128)(2,1)S(1)} %shard_map.276), channel_id=1, source_target_pairs={{0,2},{1,3},{2,0},{3,1},{4,6},{5,7},{6,4},{7,5},{8,10},{9,11},{10,... | collective-permute-start | bytes 884744 | tf_op jit(solution)/shard_map/ppermute | solution.py:43
  87.0 14.0 %collective-permute-start.25 = (bf16[2,48,768]{2,1,0:T(8,128)(2,1)S(1)}, bf16[2,48,768]{2,1,0:T(8,128)(2,1)S(1)}, u32[]{:S(2)}, u32[]{:S(2)}) collective-permute-start(bf16[2,48,768]{2,1,0:T(8,128)(2,1)S(1)} %get-tuple-element.124), channel_id=1, source_target_pairs={{0,4},{1,5},{2,6},{3,7},{4,0},{5,1},{6,2},{7,3},{8,12},{9,13},{10,... | collective-permute-start | bytes 442376 | tf_op jit(solution)/shard_map/ppermute | solution.py:43
  88.4 29.6 %collective-permute-start.18 = (bf16[272,768]{1,0:T(8,128)(2,1)S(1)}, bf16[272,768]{1,0:T(8,128)(2,1)S(1)}, u32[]{:S(2)}, u32[]{:S(2)}) collective-permute-start(bf16[272,768]{1,0:T(8,128)(2,1)S(1)} %shard_map.269), channel_id=1, source_target_pairs={{0,16},{8,24},{16,0},{24,8},{1,17},{9,25},{17,1},{25,9},{2,18},{10... | collective-permute-start | bytes 1253384 | tf_op jit(solution)/shard_map/ppermute | solution.py:43
  89.6 13.4 %collective-permute-start.33 = (bf16[48,768]{1,0:T(8,128)(2,1)S(1)}, bf16[48,768]{1,0:T(8,128)(2,1)S(1)}, u32[]{:S(2)}, u32[]{:S(2)}) collective-permute-start(bf16[48,768]{1,0:T(8,128)(2,1)S(1)} %get-tuple-element.131), channel_id=1, source_target_pairs={{0,8},{8,0},{16,24},{24,16},{1,9},{9,1},{17,25},{25,17},{2,10},{10... | collective-permute-start | bytes 221192 | tf_op jit(solution)/shard_map/ppermute | solution.py:43
  96.3 13.8 %collective-permute-start.45 = (bf16[96,768]{1,0:T(8,128)(2,1)S(1)}, bf16[96,768]{1,0:T(8,128)(2,1)S(1)}, u32[]{:S(2)}, u32[]{:S(2)}) collective-permute-start(bf16[96,768]{1,0:T(8,128)(2,1)S(1)} %shard_map.284.refs_0_), channel_id=1, source_target_pairs={{0,4},{1,5},{2,6},{3,7},{4,0},{5,1},{6,2},{7,3},{8,12},{9,13},{10,... | collective-permute-start | bytes 442376 | tf_op jit(solution)/shard_map/ppermute | solution.py:43
  110.1 15.5 %collective-permute-start.46 = (bf16[2,96,768]{2,1,0:T(8,128)(2,1)S(1)}, bf16[2,96,768]{2,1,0:T(8,128)(2,1)S(1)}, u32[]{:S(2)}, u32[]{:S(2)}) collective-permute-start(bf16[2,96,768]{2,1,0:T(8,128)(2,1)S(1)} %shard_map.285.refs_0_), channel_id=1, source_target_pairs={{0,1},{1,0},{2,3},{3,2},{4,5},{5,4},{6,7},{7,6},{8,9},{9,8},{10,11... | collective-permute-start | bytes 884744 | tf_op jit(solution)/shard_map/ppermute | solution.py:43
  111.9 17.6 %collective-permute-start.27 = (bf16[4,48,768]{2,1,0:T(8,128)(2,1)S(1)}, bf16[4,48,768]{2,1,0:T(8,128)(2,1)S(1)}, u32[]{:S(2)}, u32[]{:S(2)}) collective-permute-start(bf16[4,48,768]{2,1,0:T(8,128)(2,1)S(1)} %bitcast.21), channel_id=1, source_target_pairs={{0,2},{1,3},{2,0},{3,1},{4,6},{5,7},{6,4},{7,5},{8,10},{9,11},{10,... | collective-permute-start | bytes 884744 | tf_op jit(solution)/shard_map/ppermute | solution.py:43
  121.2 14.7 %collective-permute-start.47 = (bf16[2,96,768]{2,1,0:T(8,128)(2,1)S(1)}, bf16[2,96,768]{2,1,0:T(8,128)(2,1)S(1)}, u32[]{:S(2)}, u32[]{:S(2)}) collective-permute-start(bf16[2,96,768]{2,1,0:T(8,128)(2,1)S(1)} %shard_map.285.refs_0_), channel_id=1, source_target_pairs={{0,2},{1,3},{2,0},{3,1},{4,6},{5,7},{6,4},{7,5},{8,10},{9,11},{10,... | collective-permute-start | bytes 884744 | tf_op jit(solution)/shard_map/ppermute | solution.py:43
  124.1 26.5 %collective-permute-start.28 = (bf16[4,48,768]{2,1,0:T(8,128)(2,1)S(1)}, bf16[4,48,768]{2,1,0:T(8,128)(2,1)S(1)}, u32[]{:S(2)}, u32[]{:S(2)}) collective-permute-start(bf16[4,48,768]{2,1,0:T(8,128)(2,1)S(1)} %bitcast.22), channel_id=1, source_target_pairs={{0,1},{1,0},{2,3},{3,2},{4,5},{5,4},{6,7},{7,6},{8,9},{9,8},{10,11... | collective-permute-start | bytes 884744 | tf_op jit(solution)/shard_map/ppermute | solution.py:43
  125.6 23.4 %collective-permute-start.48 = (bf16[2,96,768]{2,1,0:T(8,128)(2,1)S(1)}, bf16[2,96,768]{2,1,0:T(8,128)(2,1)S(1)}, u32[]{:S(2)}, u32[]{:S(2)}) collective-permute-start(bf16[2,96,768]{2,1,0:T(8,128)(2,1)S(1)} %collective-permute-done.46.refs_1_), channel_id=1, source_target_pairs={{0,2},{1,3},{2,0},{3,1},{4,6},{5,7},{6,4},{7,5},{8,10},{9,11},{10,... | collective-permute-start | bytes 884744 | tf_op jit(solution)/shard_map/ppermute | solution.py:43
  129.6 21.0 %collective-permute-start.29 = (bf16[4,48,768]{2,1,0:T(8,128)(2,1)S(1)}, bf16[4,48,768]{2,1,0:T(8,128)(2,1)S(1)}, u32[]{:S(2)}, u32[]{:S(2)}) collective-permute-start(bf16[4,48,768]{2,1,0:T(8,128)(2,1)S(1)} %collective-permute-done.27.refs_1_), channel_id=1, source_target_pairs={{0,1},{1,0},{2,3},{3,2},{4,5},{5,4},{6,7},{7,6},{8,9},{9,8},{10,11... | collective-permute-start | bytes 884744 | tf_op jit(solution)/shard_map/ppermute | solution.py:43
  130.1 17.4 %collective-permute-start.38 = (bf16[208,768]{1,0:T(8,128)(2,1)S(1)}, bf16[208,768]{1,0:T(8,128)(2,1)S(1)}, u32[]{:S(2)}, u32[]{:S(2)}) collective-permute-start(bf16[208,768]{1,0:T(8,128)(2,1)S(1)} %shard_map.280.refs_0_), channel_id=1, source_target_pairs={{0,2},{1,3},{2,0},{3,1},{4,6},{5,7},{6,4},{7,5},{8,10},{9,11},{10,... | collective-permute-start | bytes 958472 | tf_op jit(solution)/shard_map/ppermute | solution.py:43
  135.9 16.4 %collective-permute-start.39 = (bf16[208,768]{1,0:T(8,128)(2,1)S(1)}, bf16[208,768]{1,0:T(8,128)(2,1)S(1)}, u32[]{:S(2)}, u32[]{:S(2)}) collective-permute-start(bf16[208,768]{1,0:T(8,128)(2,1)S(1)} %shard_map.280.refs_0_), channel_id=1, source_target_pairs={{0,1},{1,0},{2,3},{3,2},{4,5},{5,4},{6,7},{7,6},{8,9},{9,8},{10,11... | collective-permute-start | bytes 958472 | tf_op jit(solution)/shard_map/ppermute | solution.py:43
  (37 other events, 334.4 us)

commit v3 on v2

--- a/solution.py
+++ b/solution.py
@@ -106,7 +106,7 @@
 
 
 def prep_kernel(x0, x1, x2, x3, c0, c1, c2, c3, s0, s1, s2, s3, wd, wo,
-                hid1, hid1_t, hid2, hid2_t, cot, dact, datt, csum, vec, bq_own, pos, sm, bq):
+                hid1, hid1_t, hid2, hid2_t, cot, dact, datt, csum, vec, bq_own, sm, bq):
     me = lax.axis_index("shard")
     count = x0.shape[0]
     rows = wo.shape[0]
@@ -118,7 +118,6 @@
         for k in range(6):
             vec[k : k + 1, rows * s : rows * (s + 1)] = sm[s, k : k + 1, :rows]
         bq[:, 3 * rows * s : 3 * rows * (s + 1)] = sm[s, 6:7, :]
-        pos[:, count * s : count * (s + 1)] = sm[s, 7:8, :count]
     for t in range(4):
 
         @pl.when(me == t)
@@ -143,21 +142,42 @@
     csum[...] = jnp.sum(as_float(cot[...]), axis=0, keepdims=True)
 
 
-def att_kernel(order, hid, hid_t, cot, datt, q0, q1, q2, q2r, q3, q3r, bq, ca, sa, sb, segc, segr,
-               sa_o, sb_o, ka_o, kb_o, att_o, dproj_o, wfull, bsum, neg, grid):
+def mask_kernel(segc, segr, s0, s1, s2, s3, neg, ca, sa, sb):
+    me = lax.axis_index("shard")
+    col = lax.broadcasted_iota(jnp.int32, neg.shape, 1)
+    row = lax.broadcasted_iota(jnp.int32, neg.shape, 0)
+    neg[...] = jnp.where((col <= row) & (segc[...] == segr[...]), 0.0, -jnp.inf)
+    count = neg.shape[0] // 4
+    half = ROT // 2
+    freqs = jnp.exp(
+        lax.broadcasted_iota(jnp.int32, (half, count), 0).astype(F32) * (-math.log(10000.0) / half)
+    )
+    rest = jnp.zeros((HEAD_DIM - ROT, count), F32)
+    none = jnp.zeros((half, count), F32)
+    for j, ref in enumerate((s0, s1, s2, s3)):
+        place = pl.ds(pl.multiple_of((me ^ j) * count, count), count)
+        angles = ref[7:8, :count] * freqs
+        cosine, sine = jnp.cos(angles), jnp.sin(angles)
+        for out, parts in (
+            (ca, [cosine, cosine, rest + 1.0]),
+            (sa, [-sine, none, rest]),
+            (sb, [none, sine, rest]),
+        ):
+            out[place, :] = jnp.concatenate(parts + parts, axis=0).T
+
+
+def att_kernel(order, hid, hid_t, cot, datt, q0, q1, q2, q2r, q3, q3r, bq, ca, sa, sb, neg,
+               sa_o, sb_o, ka_o, kb_o, att_o, dproj_o, wfull, bsum, grid):
     me = lax.axis_index("shard")
     first, second = (bit_of("rep", bit) for bit in order)
     rows = q0.shape[0]
-    length, width = cot.shape
+    _, width = cot.shape
     two = 2 * HEAD_DIM
     n_h = rows // HEAD_DIM
     side = bit_of("rep", 1)
     for j, part, q in ((0, 0, q0), (1, 0, q1), (2, side, q2), (2, 1 - side, q2r), (3, side, q3), (3, 1 - side, q3r)):
         n = q.shape[0]
         wfull[pl.ds(pl.multiple_of((me ^ j) * rows + part * n, 16), n), :] = q[...]
-    col = lax.broadcasted_iota(jnp.int32, (length, length), 1)
-    row = lax.broadcasted_iota(jnp.int32, (length, length), 0)
-    neg[...] = jnp.where((col <= row) & (segc[...] == segr[...]), 0.0, -jnp.inf)
     proj = dot(hid[...], wfull[...], ((1,), (0,))) + bq[...]
     for h in range(n_h):
         qk = proj[:, two * h : two * (h + 1)]
@@ -438,25 +458,16 @@
         sub = rows // 4
         n_c = width // rows
 
-        hid1, hid1_t, hid2, hid2_t, cot, dact, datt, csum, vec_in, bias_qkv, position_all = call(
+        hid1, hid1_t, hid2, hid2_t, cot, dact, datt, csum, vec_in, bias_qkv = call(
             prep_kernel,
             [((length, width), BF), ((width, length), BF)] * 2
             + [((length, width), BF), ((length, wide), F32), ((length, rows), BF), ((1, width), F32)]
-            + [((8, width), F32), ((1, 3 * rows), F32), ((1, length), F32)],
+            + [((8, width), F32), ((1, 3 * rows), F32)],
             (*x, *c, *small, w_down, w_out),
             scratch=[((4, 8, 3 * rows), F32), ((1, 3 * width), F32)],
             flops=1_000_000_000,
             limit=24,
         )
-        half = ROT // 2
-        lane = jnp.arange(2 * HEAD_DIM) % HEAD_DIM
-        freqs = jnp.exp((lane % half).astype(F32) * (-math.log(10000.0) / half))
-        angles = position_all.reshape(-1, 1) * freqs[None, :]
-        cosine, sine = jnp.cos(angles), jnp.sin(angles)
-        ca = jnp.where(lane < ROT, cosine, 1.0)
-        sa = jnp.where(lane < half, -sine, 0.0)
-        sb = jnp.where((lane >= half) & (lane < ROT), sine, 0.0)
-
         *grad_a, activ, slope, wu_full = call(
             lambda *refs: mlp1_kernel(order_down, *refs),
             [((2, wide // 8, width), BF)] * 4
@@ -473,6 +484,12 @@
             scratch=[((width, wide), BF)],
             flops=2_000_000_000,
             limit=24,
+        )
+        neg, ca, sa, sb = call(
+            mask_kernel,
+            [((length, length), F32)] + [((length, 2 * HEAD_DIM), F32)] * 3,
+            (segments.reshape(-1, 1), segments, *small),
+            limit=16,
         )
         *grad_c, att, dproj, wq_full, bsum = call(
             lambda *refs: att_kernel(order_att, *refs),
@@ -483,8 +500,8 @@
                 ((width, 3 * rows), BF),
                 ((1, 3 * rows), F32),
             ],
-            (hid1, hid1_t, cot, datt, *q_w, bias_qkv, ca, sa, sb, segments.reshape(-1, 1), segments),
-            scratch=[((length, length), F32), ((width, width), BF)],
+            (hid1, hid1_t, cot, datt, *q_w, bias_qkv, ca, sa, sb, neg),
+            scratch=[((width, width), BF)],
             flops=4_000_000_000,
             limit=24,
         )

time: 159 us -> 173 us (1.088)
  waiting for transfers between devices: 66.9 us -> 82.1 us
  starting transfers between devices: 57.9 us -> 52.8 us
  local copies, waits for them, and re-layouts: 0.98 us -> 4.21 us
    ppermute x49, waiting for transfers between devices: 66.9 us -> 82.1 us  [swap(): return lax.ppermute(value, axis, [(i, i ^ bit) for i in range(size)])]
    ppermute x49, starting transfers between devices: 57.9 us -> 52.8 us  [swap(): return lax.ppermute(value, axis, [(i, i ^ bit) for i in range(size)])]
    unnamed x24 -> x32, local copies, waits for them, and re-layouts: 0.8 us -> 4.03 us
    pallas_call x24 -> x25, Pallas kernels: 27.5 us -> 28.9 us  [call(): pl.pallas_call(kernel, out_shape=shapes, scratch_shapes=[pltpu.VMEM(s, d)...]
  transfers between devices with their start and end apart: 49 -> 49, of which waited for: 19 -> 24; matrix products, arithmetic and copies ran while one was open for 2% -> 1% of each run, Pallas kernels for 9% -> 9%
where the time goes in v3:
time: 173 us; the launch traced here: 171 us
  waiting for transfers between devices  82.1 us (47%)
  starting transfers between devices  52.8 us (31%)
  Pallas kernels  28.9 us (17%)
  local copies, waits for them, and re-layouts  4.21 us (2%)
    ppermute x49, waiting for transfers between devices, swap(): return lax.ppermute(value, axis, [(i, i ^ bit) for i in range(size)])  82.1 us
    ppermute x49, starting transfers between devices, swap(): return lax.ppermute(value, axis, [(i, i ^ bit) for i in range(size)])  52.8 us
    pallas_call x25, Pallas kernels, call(): pl.pallas_call(kernel, out_shape=shapes, scratch_shapes=[pltpu.VMEM(s, d)...  28.9 us
    unnamed x32, local copies, waits for them, and re-layouts  4.03 us
  transfers between devices with their start and end apart: 49, of which 24 were waited for; matrix products, arithmetic and copies ran while one was open for 1% of the time, Pallas kernels for 9%

profile of v3, /device:TPU:0, one launch (start us, length us, event | category | flops | bytes accessed | tf_op | source)
XLA Modules:
  0.0 170.7 jit_solution(37639759321155720)
XLA Ops:
  0.7 3.0 %collective-permute-start.1 = (bf16[128,768]{1,0:T(8,128)(2,1)}, bf16[128,768]{1,0:T(8,128)(2,1)}, u32[]{:S(2)}, u32[]{:S(2)}) collective-permute-start(bf16[128,768]{1,0:T(8,128)(2,1)} %bitcast.16), channel_id=1, source_target_pairs={{0,16},{8,24},{16,0},{24,8},{1,17},{9,25},{17,1},{25,9},{2,18},{10... | collective-permute-start | bytes 589832 | tf_op jit(solution)/shard_map/ppermute | solution.py:43
  4.3 3.3 %shard_map.263 = (bf16[192,576]{1,0:T(8,128)(2,1)}, bf16[192,576]{1,0:T(8,128)(2,1)}, bf16[96,576]{1,0:T(8,128)(2,1)}, bf16[96,576]{1,0:T(8,128)(2,1)}, bf16[192...) custom-call(bf16[192,2304]{1,0:T(8,128)(2,1)} %wq.1, ...), custom_call_target="tpu_custom_call" | custom-call | bytes 3929984 | tf_op jit(solution)/shard_map/pallas_call | solution.py:53
  23.0 3.3 %shard_map.264 = (bf16[512,768]{1,0:T(8,128)(2,1)S(1)}, bf16[768,512]{1,0:T(8,128)(2,1)S(1)}, bf16[512,768]{1,0:T(8,128)(2,1)S(1)}, bf16[768,512]{1,0:T(8,128)(2...) custom-call(bf16[128,768]{1,0:T(8,128)(2,1)S(1)} %bitcast.18, ...), custom_call_target="tpu_custom_call" | custom-call | flops 1000000000 | bytes 8852736 | tf_op jit(solution)/shard_map/pallas_call | solution.py:53
  26.3 7.6 %collective-permute-done.10.refs_6_ = bf16[96,576]{1,0:T(8,128)(2,1)S(1)} collective-permute-done((bf16[96,576]{1,0:T(8,128)(2,1)}, bf16[96,576]{1,0:T(8,128)(2,1)S(1)}, u32[]{:S(2)}, u32[]{:S(2)}) %collective-permute-start.10) | collective-permute-done | bytes 110624 | tf_op jit(solution)/shard_map/ppermute | solution.py:43
  37.3 3.2 %shard_map.267 = (bf16[2,96,768]{2,1,0:T(8,128)(2,1)S(1)}, bf16[2,96,768]{2,1,0:T(8,128)(2,1)S(1)}, bf16[2,96,768]{2,1,0:T(8,128)(2,1)S(1)}, bf16[2,96,768]{2,1,...) custom-call(bf16[512,768]{1,0:T(8,128)(2,1)S(1)} %get-tuple-element.101.refs, ...), custom_call_target="tpu_custom_call" | custom-call | flops 2000000000 | bytes 7474176 | tf_op jit(solution)/shard_map/pallas_call | solution.py:53
  43.6 6.9 %shard_map.266 = (bf16[4,48,768]{2,1,0:T(8,128)(2,1)S(1)}, bf16[4,48,768]{2,1,0:T(8,128)(2,1)S(1)}, bf16[4,48,768]{2,1,0:T(8,128)(2,1)S(1)}, bf16[4,48,768]{2,1,...) custom-call(bf16[512,768]{1,0:T(8,128)(2,1)S(1)} %get-tuple-element., ...), custom_call_target="tpu_custom_call" | custom-call | flops 4000000000 | bytes 8131072 | tf_op jit(solution)/shard_map/pallas_call | solution.py:53
  50.5 4.9 %shard_map.269 = (bf16[2,272,768]{2,1,0:T(8,128)(2,1)S(1)}, bf16[2,272,768]{2,1,0:T(8,128)(2,1)S(1)}) custom-call(bf16[128,768]{1,0:T(8,128)(2,1)S(1)} %bitcast.19, bf16[128,768]{1,0:T(8,128)(2,1)} %collective-permute-done.x1, bf16[128,768]{1,0:T(8,128)(2,1)} %collective-permute-done.1.x2, bf16[128,768]{1,0:T(8,128)(2,1)S(1)} %copy-done.11, ...), custom_call_target="tpu_custom_call" | custom-call | flops 3000000000 | bytes 8388864 | tf_op jit(solution)/shard_map/pallas_call | solution.py:53
  60.9 4.6 %collective-permute-done.20.got = bf16[4,48,768]{2,1,0:T(8,128)(2,1)S(1)} collective-permute-done((bf16[4,48,768]{2,1,0:T(8,128)(2,1)S(1)}, bf16[4,48,768]{2,1,0:T(8,128)(2,1)S(1)}, u32[]{:S(2)}, u32[]{:S(2)}) %collective-permute-start.20) | collective-permute-done | bytes 294944 | tf_op jit(solution)/shard_map/ppermute | solution.py:43
  67.4 4.4 %collective-permute-done.19.got = bf16[4,48,768]{2,1,0:T(8,128)(2,1)S(1)} collective-permute-done((bf16[4,48,768]{2,1,0:T(8,128)(2,1)S(1)}, bf16[4,48,768]{2,1,0:T(8,128)(2,1)S(1)}, u32[]{:S(2)}, u32[]{:S(2)}) %collective-permute-start.19) | collective-permute-done | bytes 294944 | tf_op jit(solution)/shard_map/ppermute | solution.py:43
  73.5 4.6 %collective-permute-done.31.got = bf16[4,48,768]{2,1,0:T(8,128)(2,1)S(1)} collective-permute-done((bf16[4,48,768]{2,1,0:T(8,128)(2,1)S(1)}, bf16[4,48,768]{2,1,0:T(8,128)(2,1)S(1)}, u32[]{:S(2)}, u32[]{:S(2)}) %collective-permute-start.31) | collective-permute-done | bytes 294944 | tf_op jit(solution)/shard_map/ppermute | solution.py:43
  84.4 3.6 %collective-permute-done.41.refs_1_ = bf16[2,96,768]{2,1,0:T(8,128)(2,1)S(1)} collective-permute-done((bf16[2,96,768]{2,1,0:T(8,128)(2,1)S(1)}, bf16[2,96,768]{2,1,0:T(8,128)(2,1)S(1)}, u32[]{:S(2)}, u32[]{:S(2)}) %collective-permute-start.41) | collective-permute-done | bytes 294944 | tf_op jit(solution)/shard_map/ppermute | solution.py:43
  89.6 2.8 %collective-permute-done.32.more = bf16[4,48,768]{2,1,0:T(8,128)(2,1)S(1)} collective-permute-done((bf16[4,48,768]{2,1,0:T(8,128)(2,1)S(1)}, bf16[4,48,768]{2,1,0:T(8,128)(2,1)S(1)}, u32[]{:S(2)}, u32[]{:S(2)}) %collective-permute-start.32) | collective-permute-done | bytes 294944 | tf_op jit(solution)/shard_map/ppermute | solution.py:43
  94.4 2.7 %collective-permute-start.44 = (bf16[96,768]{1,0:T(8,128)(2,1)S(1)}, bf16[96,768]{1,0:T(8,128)(2,1)S(1)}, u32[]{:S(2)}, u32[]{:S(2)}) collective-permute-start(bf16[96,768]{1,0:T(8,128)(2,1)S(1)} %get-tuple-element.152), channel_id=1, source_target_pairs={{0,4},{1,5},{2,6},{3,7},{4,0},{5,1},{6,2},{7,3},{8,12},{9,13},{10,... | collective-permute-start | bytes 442376 | tf_op jit(solution)/shard_map/ppermute | solution.py:43
  101.1 3.6 %collective-permute-done.34.refs_2_ = bf16[48,768]{1,0:T(8,128)(2,1)S(1)} collective-permute-done((bf16[48,768]{1,0:T(8,128)(2,1)S(1)}, bf16[48,768]{1,0:T(8,128)(2,1)S(1)}, u32[]{:S(2)}, u32[]{:S(2)}) %collective-permute-start.34) | collective-permute-done | bytes 73760 | tf_op jit(solution)/shard_map/ppermute | solution.py:43
  105.6 2.8 %collective-permute-done.44.got = bf16[96,768]{1,0:T(8,128)(2,1)S(1)} collective-permute-done((bf16[96,768]{1,0:T(8,128)(2,1)S(1)}, bf16[96,768]{1,0:T(8,128)(2,1)S(1)}, u32[]{:S(2)}, u32[]{:S(2)}) %collective-permute-start.44) | collective-permute-done | bytes 147488 | tf_op jit(solution)/shard_map/ppermute | solution.py:43
  108.6 7.8 %collective-permute-done.25.got = bf16[2,48,768]{2,1,0:T(8,128)(2,1)S(1)} collective-permute-done((bf16[2,48,768]{2,1,0:T(8,128)(2,1)S(1)}, bf16[2,48,768]{2,1,0:T(8,128)(2,1)S(1)}, u32[]{:S(2)}, u32[]{:S(2)}) %collective-permute-start.25) | collective-permute-done | bytes 147488 | tf_op jit(solution)/shard_map/ppermute | solution.py:43
  116.6 2.9 %collective-permute-done.36.got = bf16[2,48,768]{2,1,0:T(8,128)(2,1)S(1)} collective-permute-done((bf16[2,48,768]{2,1,0:T(8,128)(2,1)S(1)}, bf16[2,48,768]{2,1,0:T(8,128)(2,1)S(1)}, u32[]{:S(2)}, u32[]{:S(2)}) %collective-permute-start.36) | collective-permute-done | bytes 147488 | tf_op jit(solution)/shard_map/ppermute | solution.py:43
  119.9 4.4 %collective-permute-done.45.refs_1_ = bf16[96,768]{1,0:T(8,128)(2,1)S(1)} collective-permute-done((bf16[96,768]{1,0:T(8,128)(2,1)S(1)}, bf16[96,768]{1,0:T(8,128)(2,1)S(1)}, u32[]{:S(2)}, u32[]{:S(2)}) %collective-permute-start.45) | collective-permute-done | bytes 147488 | tf_op jit(solution)/shard_map/ppermute | solution.py:43
  125.9 7.2 %collective-permute-start.47 = (bf16[2,96,768]{2,1,0:T(8,128)(2,1)S(1)}, bf16[2,96,768]{2,1,0:T(8,128)(2,1)S(1)}, u32[]{:S(2)}, u32[]{:S(2)}) collective-permute-start(bf16[2,96,768]{2,1,0:T(8,128)(2,1)S(1)} %shard_map.286.refs_0_), channel_id=1, source_target_pairs={{0,2},{1,3},{2,0},{3,1},{4,6},{5,7},{6,4},{7,5},{8,10},{9,11},{10,... | collective-permute-start | bytes 884744 | tf_op jit(solution)/shard_map/ppermute | solution.py:43
  134.2 2.9 %collective-permute-done.37.refs_1_ = bf16[112,768]{1,0:T(8,128)(2,1)S(1)} collective-permute-done((bf16[112,768]{1,0:T(8,128)(2,1)S(1)}, bf16[112,768]{1,0:T(8,128)(2,1)S(1)}, u32[]{:S(2)}, u32[]{:S(2)}) %collective-permute-start.37) | collective-permute-done | bytes 172064 | tf_op jit(solution)/shard_map/ppermute | solution.py:43
  140.9 8.1 %collective-permute-done.27.refs_1_ = bf16[4,48,768]{2,1,0:T(8,128)(2,1)S(1)} collective-permute-done((bf16[4,48,768]{2,1,0:T(8,128)(2,1)S(1)}, bf16[4,48,768]{2,1,0:T(8,128)(2,1)S(1)}, u32[]{:S(2)}, u32[]{:S(2)}) %collective-permute-start.27) | collective-permute-done | bytes 294944 | tf_op jit(solution)/shard_map/ppermute | solution.py:43
  151.3 4.5 %collective-permute-done.38.refs_1_ = bf16[208,768]{1,0:T(8,128)(2,1)S(1)} collective-permute-done((bf16[208,768]{1,0:T(8,128)(2,1)S(1)}, bf16[208,768]{1,0:T(8,128)(2,1)S(1)}, u32[]{:S(2)}, u32[]{:S(2)}) %collective-permute-start.38) | collective-permute-done | bytes 319520 | tf_op jit(solution)/shard_map/ppermute | solution.py:43
  157.3 3.5 %collective-permute-done.48.refs_3_ = bf16[2,96,768]{2,1,0:T(8,128)(2,1)S(1)} collective-permute-done((bf16[2,96,768]{2,1,0:T(8,128)(2,1)S(1)}, bf16[2,96,768]{2,1,0:T(8,128)(2,1)S(1)}, u32[]{:S(2)}, u32[]{:S(2)}) %collective-permute-start.48) | collective-permute-done | bytes 294944 | tf_op jit(solution)/shard_map/ppermute | solution.py:43
  165.6 3.4 %collective-permute-done.40.refs_3_ = bf16[208,768]{1,0:T(8,128)(2,1)S(1)} collective-permute-done((bf16[208,768]{1,0:T(8,128)(2,1)S(1)}, bf16[208,768]{1,0:T(8,128)(2,1)S(1)}, u32[]{:S(2)}, u32[]{:S(2)}) %collective-permute-start.40) | collective-permute-done | bytes 319520 | tf_op jit(solution)/shard_map/ppermute | solution.py:43
  (143 shorter events, 63.8 us)
Async XLA Ops:
  14.7 22.4 %collective-permute-start.14 = (bf16[192,768]{1,0:T(8,128)(2,1)}, bf16[192,768]{1,0:T(8,128)(2,1)}, u32[]{:S(2)}, u32[]{:S(2)}) collective-permute-start(bf16[192,768]{1,0:T(8,128)(2,1)} %get-tuple-element.103), channel_id=1, source_target_pairs={{0,8},{8,0},{16,24},{24,16},{1,9},{9,1},{17,25},{25,17},{2,10},{10... | collective-permute-start | bytes 884744 | tf_op jit(solution)/shard_map/ppermute | solution.py:43
  14.9 22.5 %collective-permute-start.15 = (bf16[192,768]{1,0:T(8,128)(2,1)}, bf16[192,768]{1,0:T(8,128)(2,1)}, u32[]{:S(2)}, u32[]{:S(2)}) collective-permute-start(bf16[192,768]{1,0:T(8,128)(2,1)} %get-tuple-element.104), channel_id=1, source_target_pairs={{0,16},{8,24},{16,0},{24,8},{1,17},{9,25},{17,1},{25,9},{2,18},{10... | collective-permute-start | bytes 884744 | tf_op jit(solution)/shard_map/ppermute | solution.py:43
  16.6 20.7 %collective-permute-start.16 = (bf16[192,768]{1,0:T(8,128)(2,1)}, bf16[192,768]{1,0:T(8,128)(2,1)}, u32[]{:S(2)}, u32[]{:S(2)}) collective-permute-start(bf16[192,768]{1,0:T(8,128)(2,1)} %get-tuple-element.105), channel_id=1, source_target_pairs={{0,24},{8,16},{16,8},{24,0},{1,25},{9,17},{17,9},{25,1},{2,26},{10... | collective-permute-start | bytes 884744 | tf_op jit(solution)/shard_map/ppermute | solution.py:43
  16.6 17.3 %collective-permute-start.10 = (bf16[96,576]{1,0:T(8,128)(2,1)}, bf16[96,576]{1,0:T(8,128)(2,1)S(1)}, u32[]{:S(2)}, u32[]{:S(2)}) collective-permute-start(bf16[96,576]{1,0:T(8,128)(2,1)} %get-tuple-element.93), channel_id=1, source_target_pairs={{0,16},{8,24},{16,0},{24,8},{1,17},{9,25},{17,1},{25,9},{2,18},{10... | collective-permute-start | bytes 331784 | tf_op jit(solution)/shard_map/ppermute | solution.py:43
  19.0 16.3 %collective-permute-start.12 = (bf16[96,576]{1,0:T(8,128)(2,1)}, bf16[96,576]{1,0:T(8,128)(2,1)S(1)}, u32[]{:S(2)}, u32[]{:S(2)}) collective-permute-start(bf16[96,576]{1,0:T(8,128)(2,1)} %get-tuple-element.94), channel_id=1, source_target_pairs={{0,24},{8,16},{16,8},{24,0},{1,25},{9,17},{17,9},{25,1},{2,26},{10... | collective-permute-start | bytes 331784 | tf_op jit(solution)/shard_map/ppermute | solution.py:43
  55.4 24.9 %collective-permute-start.17 = (bf16[2,272,768]{2,1,0:T(8,128)(2,1)S(1)}, bf16[2,272,768]{2,1,0:T(8,128)(2,1)S(1)}, u32[]{:S(2)}, u32[]{:S(2)}) collective-permute-start(bf16[2,272,768]{2,1,0:T(8,128)(2,1)S(1)} %get-tuple-element.119), channel_id=1, source_target_pairs={{0,8},{8,0},{16,24},{24,16},{1,9},{9,1},{17,25},{25,17},{2,10},{10... | collective-permute-start | bytes 2506760 | tf_op jit(solution)/shard_map/ppermute | solution.py:43
  57.3 14.5 %collective-permute-start.19 = (bf16[4,48,768]{2,1,0:T(8,128)(2,1)S(1)}, bf16[4,48,768]{2,1,0:T(8,128)(2,1)S(1)}, u32[]{:S(2)}, u32[]{:S(2)}) collective-permute-start(bf16[4,48,768]{2,1,0:T(8,128)(2,1)S(1)} %get-tuple-element.121), channel_id=1, source_target_pairs={{0,1},{1,0},{2,3},{3,2},{4,5},{5,4},{6,7},{7,6},{8,9},{9,8},{10,11... | collective-permute-start | bytes 884744 | tf_op jit(solution)/shard_map/ppermute | solution.py:43
  57.6 20.5 %collective-permute-start.31 = (bf16[4,48,768]{2,1,0:T(8,128)(2,1)S(1)}, bf16[4,48,768]{2,1,0:T(8,128)(2,1)S(1)}, u32[]{:S(2)}, u32[]{:S(2)}) collective-permute-start(bf16[4,48,768]{2,1,0:T(8,128)(2,1)S(1)} %get-tuple-element.135), channel_id=1, source_target_pairs={{0,1},{1,0},{2,3},{3,2},{4,5},{5,4},{6,7},{7,6},{8,9},{9,8},{10,11... | collective-permute-start | bytes 884744 | tf_op jit(solution)/shard_map/ppermute | solution.py:43
  59.3 20.6 %collective-permute-start.42 = (bf16[2,96,768]{2,1,0:T(8,128)(2,1)S(1)}, bf16[2,96,768]{2,1,0:T(8,128)(2,1)S(1)}, u32[]{:S(2)}, u32[]{:S(2)}) collective-permute-start(bf16[2,96,768]{2,1,0:T(8,128)(2,1)S(1)} %get-tuple-element.150), channel_id=1, source_target_pairs={{0,2},{1,3},{2,0},{3,1},{4,6},{5,7},{6,4},{7,5},{8,10},{9,11},{10,... | collective-permute-start | bytes 884744 | tf_op jit(solution)/shard_map/ppermute | solution.py:43
  65.5 16.7 %collective-permute-start.21 = (bf16[4,48,768]{2,1,0:T(8,128)(2,1)S(1)}, bf16[4,48,768]{2,1,0:T(8,128)(2,1)S(1)}, u32[]{:S(2)}, u32[]{:S(2)}) collective-permute-start(bf16[4,48,768]{2,1,0:T(8,128)(2,1)S(1)} %shard_map.271), channel_id=1, source_target_pairs={{0,2},{1,3},{2,0},{3,1},{4,6},{5,7},{6,4},{7,5},{8,10},{9,11},{10,... | collective-permute-start | bytes 884744 | tf_op jit(solution)/shard_map/ppermute | solution.py:43
  82.3 34.2 %collective-permute-start.18 = (bf16[272,768]{1,0:T(8,128)(2,1)S(1)}, bf16[272,768]{1,0:T(8,128)(2,1)S(1)}, u32[]{:S(2)}, u32[]{:S(2)}) collective-permute-start(bf16[272,768]{1,0:T(8,128)(2,1)S(1)} %shard_map.270), channel_id=1, source_target_pairs={{0,16},{8,24},{16,0},{24,8},{1,17},{9,25},{17,1},{25,9},{2,18},{10... | collective-permute-start | bytes 1253384 | tf_op jit(solution)/shard_map/ppermute | solution.py:43
  94.4 14.0 %collective-permute-start.44 = (bf16[96,768]{1,0:T(8,128)(2,1)S(1)}, bf16[96,768]{1,0:T(8,128)(2,1)S(1)}, u32[]{:S(2)}, u32[]{:S(2)}) collective-permute-start(bf16[96,768]{1,0:T(8,128)(2,1)S(1)} %get-tuple-element.152), channel_id=1, source_target_pairs={{0,4},{1,5},{2,6},{3,7},{4,0},{5,1},{6,2},{7,3},{8,12},{9,13},{10,... | collective-permute-start | bytes 442376 | tf_op jit(solution)/shard_map/ppermute | solution.py:43
  97.4 18.9 %collective-permute-start.25 = (bf16[2,48,768]{2,1,0:T(8,128)(2,1)S(1)}, bf16[2,48,768]{2,1,0:T(8,128)(2,1)S(1)}, u32[]{:S(2)}, u32[]{:S(2)}) collective-permute-start(bf16[2,48,768]{2,1,0:T(8,128)(2,1)S(1)} %get-tuple-element.130), channel_id=1, source_target_pairs={{0,4},{1,5},{2,6},{3,7},{4,0},{5,1},{6,2},{7,3},{8,12},{9,13},{10,... | collective-permute-start | bytes 442376 | tf_op jit(solution)/shard_map/ppermute | solution.py:43
  105.2 14.3 %collective-permute-start.36 = (bf16[2,48,768]{2,1,0:T(8,128)(2,1)S(1)}, bf16[2,48,768]{2,1,0:T(8,128)(2,1)S(1)}, u32[]{:S(2)}, u32[]{:S(2)}) collective-permute-start(bf16[2,48,768]{2,1,0:T(8,128)(2,1)S(1)} %get-tuple-element.141), channel_id=1, source_target_pairs={{0,4},{1,5},{2,6},{3,7},{4,0},{5,1},{6,2},{7,3},{8,12},{9,13},{10,... | collective-permute-start | bytes 442376 | tf_op jit(solution)/shard_map/ppermute | solution.py:43
  108.5 15.8 %collective-permute-start.45 = (bf16[96,768]{1,0:T(8,128)(2,1)S(1)}, bf16[96,768]{1,0:T(8,128)(2,1)S(1)}, u32[]{:S(2)}, u32[]{:S(2)}) collective-permute-start(bf16[96,768]{1,0:T(8,128)(2,1)S(1)} %shard_map.285.refs_0_), channel_id=1, source_target_pairs={{0,4},{1,5},{2,6},{3,7},{4,0},{5,1},{6,2},{7,3},{8,12},{9,13},{10,... | collective-permute-start | bytes 442376 | tf_op jit(solution)/shard_map/ppermute | solution.py:43
  116.4 16.7 %collective-permute-start.26 = (bf16[2,48,768]{2,1,0:T(8,128)(2,1)S(1)}, bf16[2,48,768]{2,1,0:T(8,128)(2,1)S(1)}, u32[]{:S(2)}, u32[]{:S(2)}) collective-permute-start(bf16[2,48,768]{2,1,0:T(8,128)(2,1)S(1)} %shard_map.274.refs_0_), channel_id=1, source_target_pairs={{0,4},{1,5},{2,6},{3,7},{4,0},{5,1},{6,2},{7,3},{8,12},{9,13},{10,... | collective-permute-start | bytes 442376 | tf_op jit(solution)/shard_map/ppermute | solution.py:43
  119.5 17.6 %collective-permute-start.37 = (bf16[112,768]{1,0:T(8,128)(2,1)S(1)}, bf16[112,768]{1,0:T(8,128)(2,1)S(1)}, u32[]{:S(2)}, u32[]{:S(2)}) collective-permute-start(bf16[112,768]{1,0:T(8,128)(2,1)S(1)} %shard_map.280.refs_0_), channel_id=1, source_target_pairs={{0,4},{1,5},{2,6},{3,7},{4,0},{5,1},{6,2},{7,3},{8,12},{9,13},{10,... | collective-permute-start | bytes 516104 | tf_op jit(solution)/shard_map/ppermute | solution.py:43
  124.3 15.2 %collective-permute-start.46 = (bf16[2,96,768]{2,1,0:T(8,128)(2,1)S(1)}, bf16[2,96,768]{2,1,0:T(8,128)(2,1)S(1)}, u32[]{:S(2)}, u32[]{:S(2)}) collective-permute-start(bf16[2,96,768]{2,1,0:T(8,128)(2,1)S(1)} %shard_map.286.refs_0_), channel_id=1, source_target_pairs={{0,1},{1,0},{2,3},{3,2},{4,5},{5,4},{6,7},{7,6},{8,9},{9,8},{10,11... | collective-permute-start | bytes 884744 | tf_op jit(solution)/shard_map/ppermute | solution.py:43
  125.9 23.9 %collective-permute-start.47 = (bf16[2,96,768]{2,1,0:T(8,128)(2,1)S(1)}, bf16[2,96,768]{2,1,0:T(8,128)(2,1)S(1)}, u32[]{:S(2)}, u32[]{:S(2)}) collective-permute-start(bf16[2,96,768]{2,1,0:T(8,128)(2,1)S(1)} %shard_map.286.refs_0_), channel_id=1, source_target_pairs={{0,2},{1,3},{2,0},{3,1},{4,6},{5,7},{6,4},{7,5},{8,10},{9,11},{10,... | collective-permute-start | bytes 884744 | tf_op jit(solution)/shard_map/ppermute | solution.py:43
  133.1 15.9 %collective-permute-start.27 = (bf16[4,48,768]{2,1,0:T(8,128)(2,1)S(1)}, bf16[4,48,768]{2,1,0:T(8,128)(2,1)S(1)}, u32[]{:S(2)}, u32[]{:S(2)}) collective-permute-start(bf16[4,48,768]{2,1,0:T(8,128)(2,1)S(1)} %bitcast.20), channel_id=1, source_target_pairs={{0,2},{1,3},{2,0},{3,1},{4,6},{5,7},{6,4},{7,5},{8,10},{9,11},{10,... | collective-permute-start | bytes 884744 | tf_op jit(solution)/shard_map/ppermute | solution.py:43
  137.1 18.7 %collective-permute-start.38 = (bf16[208,768]{1,0:T(8,128)(2,1)S(1)}, bf16[208,768]{1,0:T(8,128)(2,1)S(1)}, u32[]{:S(2)}, u32[]{:S(2)}) collective-permute-start(bf16[208,768]{1,0:T(8,128)(2,1)S(1)} %shard_map.281.refs_0_), channel_id=1, source_target_pairs={{0,2},{1,3},{2,0},{3,1},{4,6},{5,7},{6,4},{7,5},{8,10},{9,11},{10,... | collective-permute-start | bytes 958472 | tf_op jit(solution)/shard_map/ppermute | solution.py:43
  137.9 24.5 %collective-permute-start.28 = (bf16[4,48,768]{2,1,0:T(8,128)(2,1)S(1)}, bf16[4,48,768]{2,1,0:T(8,128)(2,1)S(1)}, u32[]{:S(2)}, u32[]{:S(2)}) collective-permute-start(bf16[4,48,768]{2,1,0:T(8,128)(2,1)S(1)} %bitcast.21), channel_id=1, source_target_pairs={{0,1},{1,0},{2,3},{3,2},{4,5},{5,4},{6,7},{7,6},{8,9},{9,8},{10,11... | collective-permute-start | bytes 884744 | tf_op jit(solution)/shard_map/ppermute | solution.py:43
  139.4 21.4 %collective-permute-start.48 = (bf16[2,96,768]{2,1,0:T(8,128)(2,1)S(1)}, bf16[2,96,768]{2,1,0:T(8,128)(2,1)S(1)}, u32[]{:S(2)}, u32[]{:S(2)}) collective-permute-start(bf16[2,96,768]{2,1,0:T(8,128)(2,1)S(1)} %collective-permute-done.46.refs_1_), channel_id=1, source_target_pairs={{0,2},{1,3},{2,0},{3,1},{4,6},{5,7},{6,4},{7,5},{8,10},{9,11},{10,... | collective-permute-start | bytes 884744 | tf_op jit(solution)/shard_map/ppermute | solution.py:43
  149.7 15.9 %collective-permute-start.39 = (bf16[208,768]{1,0:T(8,128)(2,1)S(1)}, bf16[208,768]{1,0:T(8,128)(2,1)S(1)}, u32[]{:S(2)}, u32[]{:S(2)}) collective-permute-start(bf16[208,768]{1,0:T(8,128)(2,1)S(1)} %shard_map.281.refs_0_), channel_id=1, source_target_pairs={{0,1},{1,0},{2,3},{3,2},{4,5},{5,4},{6,7},{7,6},{8,9},{9,8},{10,11... | collective-permute-start | bytes 958472 | tf_op jit(solution)/shard_map/ppermute | solution.py:43
  (41 other events, 364.6 us)
